TPU v7x, 128 devices: a whole 4x4x4 slice. The times are simulated.
128 devices in a mesh: tok: 8 (over x, z_hi), feat: 16 (over y, z_lo, core).
Axes of the slice: x: 4, y: 4, z: 4 (z_hi: 2, z_lo: 2; z = z_hi * 2 + z_lo), core: 2. Of those that a mesh axis runs over, the one named last changes fastest.
Arguments:
- resid: bfloat16 [2048, 8192], P(None, ('tok', 'feat')), may hold values from -6 to 6
- resid_grad: bfloat16 [2048, 8192], P(None, ('tok', 'feat')), may hold values from -6 to 6
- active: int32 [16, 20], P('tok'), may hold values from 0 to 79, all different within a row
- w_enc: bfloat16 [8192, 10240], P(None, 'feat'), may hold values from -0.0625 to 0.0625
- b_enc: float32 [10240], P('feat'), may hold values from -3 to 3
- w_dec: bfloat16 [10240, 8192], P('feat'), may hold values from -0.25 to 0.25
- b_dec: float32 [8192], P('feat'), may hold values from -3 to 3
Outputs:
- feature_attr: float32 [2048, 10240], P('tok', 'feat')
- error: float32 [2048, 8192], P('tok', 'feat')
- error_attr: float32 [2048], P('tok')
Inputs may be any that keep to these rules, and one draw needn't show every extreme that they name: `active`: each row lists 20 different feature blocks; every block is listed by some tile.
All inputs are finite; a program needn't handle non-finite values.
Results may differ from a plain program's by a relative error of at most 0.012.
Values may be sent and summed in bfloat16 or wider, within the bound.
A program may use at most 128 MiB of HBM per device.

v0:
```python
import jax
import jax.numpy as jnp
from jax import lax
from jax.sharding import PartitionSpec as P

BLOCK = 128
TILE = 128


def per_device(resid, resid_grad, active, w_enc, b_enc, w_dec, b_dec):
    n_feat = lax.axis_size("feat")
    width = resid.shape[1]
    cols_x, cols_g = (
        lax.all_gather(resid[:, None, :], "feat", axis=1, tiled=True),
        lax.all_gather(resid_grad[:, None, :], "feat", axis=1, tiled=True),
    )
    total = cols_x.shape[0]
    cols_x = cols_x.reshape(total, n_feat * width)
    cols_g = cols_g.reshape(total, n_feat * width)
    rows_x, rows_g = (
        lax.all_to_all(cols_x, "tok", split_axis=0, concat_axis=1, tiled=True),
        lax.all_to_all(cols_g, "tok", split_axis=0, concat_axis=1, tiled=True),
    )
    tok_rows = rows_x.shape[0]
    feat_dev = w_enc.shape[1]
    blocks = feat_dev // BLOCK
    tiles_dev = active.shape[0]
    block_ids = lax.axis_index("feat") * blocks + jnp.arange(blocks, dtype=jnp.int32)
    hits = jnp.any(active[:, :, None] == block_ids[None, None, :], axis=1).astype(jnp.float32)
    pre = jnp.dot(rows_x, w_enc, preferred_element_type=jnp.float32) + b_enc
    shaped = jnp.maximum(pre, 0.0).reshape(tiles_dev, TILE, blocks, BLOCK) * hits[:, None, :, None]
    acts = shaped.reshape(tok_rows, feat_dev).astype(jnp.bfloat16)
    partial_recon = jnp.dot(acts, w_dec, preferred_element_type=jnp.float32)
    recon_share = lax.psum_scatter(
        partial_recon.astype(jnp.bfloat16), "feat", scatter_dimension=1, tiled=True
    ).astype(jnp.float32)
    share = recon_share.shape[1]
    start = lax.axis_index("feat") * share
    own_x = lax.dynamic_slice_in_dim(rows_x, start, share, 1)
    own_g = lax.dynamic_slice_in_dim(rows_g, start, share, 1)
    recon = recon_share + b_dec
    error = own_x.astype(jnp.float32) - recon
    local_terms = jnp.sum(error * own_g.astype(jnp.float32), axis=1)
    error_attr = lax.psum(local_terms, "feat")
    proj = lax.dot_general(
        rows_g, w_dec, (((1,), (1,)), ((), ())), preferred_element_type=jnp.float32
    )
    feature_attr = acts.astype(jnp.float32) * proj
    return (feature_attr, error, error_attr)


def solution(mesh):
    placed = (
        P(None, ("tok", "feat")),
        P(None, ("tok", "feat")),
        P("tok", None),
        P(None, "feat"),
        P("feat"),
        P("feat", None),
        P("feat"),
    )
    return jax.shard_map(
        per_device,
        mesh=mesh,
        in_specs=placed,
        out_specs=(P("tok", "feat"), P("tok", "feat"), P("tok")),
        check_vma=False,
    )
```

profile of v0, /device:TPU:0, one launch (start us, length us, event | category | flops | bytes accessed | tf_op | source)
XLA Modules:
  0.0 284.6 jit_solution(3607693962824944712)
XLA Ops:
  7.2 0.0 all-gather.5.cloned.1.call-start
  7.2 0.7 all-gather.5.cloned.1.call-update
  7.9 0.0 all-gather.7.cloned.1.call-start
  7.9 0.7 all-gather.7.cloned.1.call-update
  8.6 40.8 %all-gather.5.cloned.1.call-done = bf16[2048,1024]{0,1:T(8,128)(2,1)} async-done(((bf16[2048,64]{0,1:T(8,128)(2,1)}), bf16[2048,1024]{0,1:T(8,128)(2,1)}) %all-gather.5.cloned.1.call-update) | async-done | bytes 4194320 | tf_op jit(solution)/shard_map/all_gather | solution.py:14
  49.5 6.4 %copy.20 = bf16[2048,1024]{1,0:T(8,128)(2,1)} copy(bf16[2048,1024]{0,1:T(8,128)(2,1)} %all-gather.5.cloned.1.call-done) | data formatting | bytes 8388608 | tf_op jit(solution)/shard_map/all_gather | solution.py:14
  55.8 0.0 copy-start.3
  55.8 6.6 %all-to-all-start = ((bf16[8,256,1024]{2,1,0:T(8,128)(2,1)}), bf16[8,256,1024]{2,1,0:T(8,128)(2,1)}, u32[]{:S(2)}, u32[]{:S(2)}) async-start(bf16[8,256,1024]{2,1,0:T(8,128)(2,1)} %bitcast.21), calls=%async_computation | async-start | bytes 8388608 | tf_op jit(solution)/shard_map/all_to_all | solution.py:21
  62.5 0.0 reduce-scatter.2.cloned.1.call-start
  62.5 0.0 copy-done.3
  62.5 0.2 compare_reduce_fusion
  62.7 0.1 copy.22
  62.8 0.2 mul.24
  63.1 0.2 copy.23
  63.4 59.7 %all-to-all-done = bf16[8,256,1024]{2,1,0:T(8,128)(2,1)} async-done(((bf16[8,256,1024]{2,1,0:T(8,128)(2,1)}), bf16[8,256,1024]{2,1,0:T(8,128)(2,1)}, u32[]{:S(2)}, u32[]{:S(2)}) %all-to-all-start) | async-done | bytes 4194336 | tf_op jit(solution)/shard_map/all_to_all | solution.py:21
  123.1 0.0 copy-start.4
  123.1 0.0 slice-start
  123.1 2.9 %copy.26 = bf16[8,32,8,1024]{3,2,0,1:T(8,128)(2,1)S(1)} copy(bf16[8,32,8,1024]{3,2,1,0:T(8,128)(2,1)} %bitcast.4) | data formatting | bytes 8388608 | tf_op jit(solution)/shard_map/all_to_all | solution.py:21
  126.0 0.0 copy-start
  126.0 2.0 copy-done
  127.9 0.0 copy-done.4
  127.9 0.0 slice-start.1
  127.9 0.0 slice-start.2
  127.9 6.5 %fusion.2 = bf16[256,640]{1,0:T(8,128)(2,1)S(1)} fusion(f32[256,640]{1,0:T(8,128)S(1)} %copy.23, bf16[256,8192]{1,0:T(8,128)(2,1)S(1)} %bitcast.23, bf16[8192,640]{1,0:T(8,128)(2,1)} %param.10, f32[640]{0:T(1024)S(1)} %copy-done.4), kind=kOutput, calls=%fused_computation.5 | convolution fusion | flops 2685009920 | bytes 15665664 | tf_op jit(solution)/shard_map/dot_general | solution.py:30
  134.4 0.0 slice-done
  134.4 0.0 slice-done.1
  134.4 0.0 slice-done.2
  134.4 4.9 %convolution_convert_fusion = bf16[256,8192]{1,0:T(8,128)(2,1)} fusion(bf16[256,640]{1,0:T(8,128)(2,1)S(1)} %fusion.2, bf16[640,8192]{1,0:T(8,128)(2,1)S(1)} %bitcast.30), kind=kOutput, calls=%fused_computation | convolution fusion | flops 2686451712 | bytes 15007744 | tf_op jit(solution)/shard_map/dot_general | solution.py:33
  139.4 0.0 reduce-scatter.2.cloned.1.call-update
  139.4 0.0 all-gather.7.cloned.1.call-done
  139.4 6.4 %copy.24 = bf16[2048,1024]{1,0:T(8,128)(2,1)} copy(bf16[2048,1024]{0,1:T(8,128)(2,1)} %all-gather.7.cloned.1.call-done) | data formatting | bytes 8388608 | tf_op jit(solution)/shard_map/all_gather | solution.py:15
  145.8 4.8 %all-to-all-start.1 = ((bf16[8,256,1024]{2,1,0:T(8,128)(2,1)}), bf16[8,256,1024]{2,1,0:T(8,128)(2,1)}, u32[]{:S(2)}, u32[]{:S(2)}) async-start(bf16[8,256,1024]{2,1,0:T(8,128)(2,1)} %bitcast.22), calls=%async_computation.1 | async-start | bytes 8388608 | tf_op jit(solution)/shard_map/all_to_all | solution.py:22
  150.6 61.9 %all-to-all-done.1 = bf16[8,256,1024]{2,1,0:T(8,128)(2,1)} async-done(((bf16[8,256,1024]{2,1,0:T(8,128)(2,1)}), bf16[8,256,1024]{2,1,0:T(8,128)(2,1)}, u32[]{:S(2)}, u32[]{:S(2)}) %all-to-all-start.1) | async-done | bytes 4194336 | tf_op jit(solution)/shard_map/all_to_all | solution.py:22
  212.5 2.7 copy.27
  215.2 0.0 copy-start.1
  215.2 1.9 copy-done.1
  217.1 0.0 copy-start.2
  217.1 7.1 %convolution_multiply_fusion = f32[256,640]{1,0:T(8,128)} fusion(bf16[256,8192]{1,0:T(8,128)(2,1)S(1)} %bitcast.25, bf16[640,8192]{1,0:T(8,128)(2,1)} %param.12, bf16[256,640]{1,0:T(8,128)(2,1)S(1)} %fusion.2), kind=kOutput, calls=%fused_computation.1 | convolution fusion | flops 2684682240 | bytes 15663104 | tf_op jit(solution)/shard_map/dot_general | solution.py:45
  224.2 22.1 %reduce-scatter.2.cloned.1.call-done = bf16[256,512]{1,0:T(8,128)(2,1)} async-done(((bf16[256,8192]{1,0:T(8,128)(2,1)}), bf16[256,512]{1,0:T(8,128)(2,1)}) %reduce-scatter.2.cloned.1.call-update) | async-done | bytes 262160 | tf_op jit(solution)/shard_map/reduce_scatter | solution.py:34
  246.3 0.0 copy-done.2
  246.3 2.0 multiply_reduce_fusion
  248.3 29.7 %psum.7 = f32[256]{0:T(256)} all-reduce(f32[256]{0:T(256)S(1)} %get-tuple-element.3), channel_id=1, replica_groups=mesh['tok'=8,'feat'=16] {'feat'}, use_global_device_ids=true, to_apply=%region_3.0 | all-reduce | flops 256 | bytes 2048 | tf_op jit(solution)/shard_map/psum | solution.py:44
  (4 shorter events, 0.1 us)
Async XLA Ops:
  7.2 42.3 %all-gather.5.cloned.1.call-start = ((), (), s32[]{:S(2)}) async-start(), calls=%async_computation.4 | async-start | bytes 4456448 | tf_op jit(solution)/shard_map/all_gather | solution.py:14
  7.9 131.5 %all-gather.7.cloned.1.call-start = ((), (), s32[]{:S(2)}) async-start(), calls=%async_computation.5 | async-start | bytes 4456448 | tf_op jit(solution)/shard_map/all_gather | solution.py:15
  55.8 6.7 %copy-start.3 = (s32[2,20]{1,0:T(2,128)S(1)}, s32[2,20]{1,0:T(2,128)}, u32[]{:S(2)}) copy-start(s32[2,20]{1,0:T(2,128)} %param.9) | copy-start | bytes 484
  55.8 67.2 %all-to-all-start = ((bf16[8,256,1024]{2,1,0:T(8,128)(2,1)}), bf16[8,256,1024]{2,1,0:T(8,128)(2,1)}, u32[]{:S(2)}, u32[]{:S(2)}) async-start(bf16[8,256,1024]{2,1,0:T(8,128)(2,1)} %bitcast.21), calls=%async_computation | async-start | bytes 8388608 | tf_op jit(solution)/shard_map/all_to_all | solution.py:21
  62.5 183.8 %reduce-scatter.2.cloned.1.call-start = ((), (), s32[]{:S(2)}) async-start(), calls=%async_computation.3 | async-start | bytes 4456448 | tf_op jit(solution)/shard_map/reduce_scatter | solution.py:34
  123.1 4.9 %copy-start.4 = (f32[640]{0:T(1024)S(1)}, f32[640]{0:T(1024)}, u32[]{:S(2)}) copy-start(f32[640]{0:T(1024)} %param.11) | copy-start | bytes 7684
  123.1 11.3 %slice-start = ((s8[10485760]{0:T(1024)(128)(4,1)}), s8[4194304]{0:T(1024)(128)(4,1)S(1)}, s32[]{:S(2)}) async-start(s8[10485760]{0:T(1024)(128)(4,1)} %bitcast.29), calls=%async_computation.6 | async-start | bytes 8388608
  126.0 2.0 copy-start
  127.9 6.5 %slice-start.1 = ((s8[10485760]{0:T(1024)(128)(4,1)}), s8[4194304]{0:T(1024)(128)(4,1)S(1)}, s32[]{:S(2)}) async-start(s8[10485760]{0:T(1024)(128)(4,1)} %bitcast.29), calls=%async_computation.7 | async-start | bytes 8388608
  127.9 6.5 %slice-start.2 = ((s8[10485760]{0:T(1024)(128)(4,1)}), s8[2097152]{0:T(1024)(128)(4,1)S(1)}, s32[]{:S(2)}) async-start(s8[10485760]{0:T(1024)(128)(4,1)} %bitcast.29), calls=%async_computation.8 | async-start | bytes 4194304
  145.8 66.7 %all-to-all-start.1 = ((bf16[8,256,1024]{2,1,0:T(8,128)(2,1)}), bf16[8,256,1024]{2,1,0:T(8,128)(2,1)}, u32[]{:S(2)}, u32[]{:S(2)}) async-start(bf16[8,256,1024]{2,1,0:T(8,128)(2,1)} %bitcast.22), calls=%async_computation.1 | async-start | bytes 8388608 | tf_op jit(solution)/shard_map/all_to_all | solution.py:22
  215.2 1.9 copy-start.1
  217.1 29.2 %copy-start.2 = (f32[512]{0:T(512)S(1)}, f32[512]{0:T(512)}, u32[]{:S(2)}) copy-start(f32[512]{0:T(512)} %param.13) | copy-start | bytes 6148
Sparse Core Ops, SparseCore 0:
  9.7 39.7 all-gather.4
  51.2 79.7 all-gather.6
  139.5 106.7 reduce-scatter.1
where the time goes:
time: 285 us
  waiting for transfers between devices  186 us (65%)
  blocking collectives  29.7 us (10%)
  local copies, waits for them, and re-layouts  22.8 us (8%)
  matrix products  18.5 us (6%)
  between operations  13.9 us (5%)
  starting transfers between devices  11.6 us (4%)
    all_to_all x1, waiting for transfers between devices, per_device(): lax.all_to_all(cols_g, 'tok', split_axis=0, concat_axis=1, tiled=True)  61.9 us
    all_to_all x1, waiting for transfers between devices, per_device(): lax.all_to_all(cols_x, 'tok', split_axis=0, concat_axis=1, tiled=True)  59.7 us
    all_gather x1, waiting for transfers between devices, per_device(): lax.all_gather(resid[:, None, :], 'feat', axis=1, tiled=True)  40.8 us
    psum x1, blocking collectives, per_device(): error_attr = lax.psum(local_terms, 'feat')  29.7 us
    reduce_scatter x1, waiting for transfers between devices, per_device(): lax.psum_scatter(partial_recon.astype(jnp.bfloat16), 'feat', scatter_dime...  22.1 us
    dot_general x1, matrix products, per_device(): lax.dot_general(rows_g, w_dec, (((1,), (1,)), ((), ())), preferred_elemen...  7.11 us
    all_to_all x1, starting transfers between devices, per_device(): lax.all_to_all(cols_x, 'tok', split_axis=0, concat_axis=1, tiled=True)  6.65 us
    dot_general x1, matrix products, per_device(): pre = jnp.dot(rows_x, w_enc, preferred_element_type=jnp.float32) + b_enc  6.46 us
  transfers between devices with their start and end apart: 5, of which 4 were waited for; matrix products, arithmetic and copies ran while one was open for 13% of the time, Pallas kernels for 0%

commit v1 on v0

v1 whole, which is shorter than its diff:
```python
import jax
import jax.numpy as jnp
from jax import lax
from jax.sharding import PartitionSpec as P

BLOCK = 128
TILE = 128


def gather_rows(part):
    n_tok = lax.axis_size("tok")
    total, width = part.shape
    own = part.T.reshape(width, n_tok, total // n_tok).transpose(1, 0, 2)
    own = lax.all_to_all(own, "tok", split_axis=0, concat_axis=0, tiled=True)
    cols = lax.all_gather(own, "feat", axis=1, tiled=False)
    return cols.reshape(-1, total // n_tok)


def per_device(resid, resid_grad, active, w_enc, b_enc, w_dec, b_dec):
    rows_x = gather_rows(resid)
    rows_g = gather_rows(resid_grad)
    tok_rows = rows_x.shape[1]
    feat_dev = w_enc.shape[1]
    blocks = feat_dev // BLOCK
    tiles_dev = active.shape[0]
    block_ids = lax.axis_index("feat") * blocks + jnp.arange(blocks, dtype=jnp.int32)
    hits = jnp.any(active[:, :, None] == block_ids[None, None, :], axis=1).astype(jnp.float32)
    pre = lax.dot_general(rows_x, w_enc, (((0,), (0,)), ((), ())), preferred_element_type=jnp.float32) + b_enc
    shaped = jnp.maximum(pre, 0.0).reshape(tiles_dev, TILE, blocks, BLOCK) * hits[:, None, :, None]
    acts = shaped.reshape(tok_rows, feat_dev).astype(jnp.bfloat16)
    partial_recon = jnp.dot(acts, w_dec, preferred_element_type=jnp.float32)
    recon_share = lax.psum_scatter(
        partial_recon.astype(jnp.bfloat16), "feat", scatter_dimension=1, tiled=True
    ).astype(jnp.float32)
    share = recon_share.shape[1]
    start = lax.axis_index("feat") * share
    own_x = lax.dynamic_slice_in_dim(rows_x, start, share, 0).T
    own_g = lax.dynamic_slice_in_dim(rows_g, start, share, 0).T
    recon = recon_share + b_dec
    error = own_x.astype(jnp.float32) - recon
    local_terms = jnp.sum(error * own_g.astype(jnp.float32), axis=1)
    error_attr = lax.psum(local_terms, "feat")
    proj = lax.dot_general(
        rows_g, w_dec, (((0,), (1,)), ((), ())), preferred_element_type=jnp.float32
    )
    feature_attr = acts.astype(jnp.float32) * proj
    return (feature_attr, error, error_attr)


def solution(mesh):
    placed = (
        P(None, ("tok", "feat")),
        P(None, ("tok", "feat")),
        P("tok", None),
        P(None, "feat"),
        P("feat"),
        P("feat", None),
        P("feat"),
    )
    return jax.shard_map(
        per_device,
        mesh=mesh,
        in_specs=placed,
        out_specs=(P("tok", "feat"), P("tok", "feat"), P("tok")),
        check_vma=False,
    )
```

time: 285 us -> 208 us (0.73)
  waiting for transfers between devices: 186 us -> 80.7 us
  blocking collectives: 29.7 us -> 55.6 us
  local copies, waits for them, and re-layouts: 22.8 us -> 36.4 us
  starting transfers between devices: 11.6 us -> 0.12 us
    all_to_all x2 -> x0, waiting for transfers between devices: 122 us -> none  [the longest x1 61.9 us: per_device(): lax.all_to_all(cols_g, 'tok', split_axis=0, concat_axis=1, tiled=True)]
    all_to_all x0 -> x2, blocking collectives: none -> 27.3 us  [gather_rows(): own = lax.all_to_all(own, 'tok', split_axis=0, concat_axis=0, tiled=True)]
    reduce_scatter x1, waiting for transfers between devices: 22.1 us -> 47.6 us  [per_device(): lax.psum_scatter(partial_recon.astype(jnp.bfloat16), 'feat', scatter_dime...]
    unnamed x17 -> x21, local copies, waits for them, and re-layouts: 3.97 us -> 19.2 us
    all_to_all x2 -> x0, starting transfers between devices: 11.4 us -> none  [the longest x1 6.65 us: per_device(): lax.all_to_all(cols_x, 'tok', split_axis=0, concat_axis=1, tiled=True)]
    all_gather x2, waiting for transfers between devices: 40.8 us -> 33.1 us  [gather_rows(): cols = lax.all_gather(own, 'feat', axis=1, tiled=False)]
    all_to_all x2, local copies, waits for them, and re-layouts: 5.54 us -> 1.7 us  [gather_rows(): own = lax.all_to_all(own, 'tok', split_axis=0, concat_axis=0, tiled=True)]
  transfers between devices with their start and end apart: 5 -> 3, of which waited for: 4 -> 3; matrix products, arithmetic and copies ran while one was open for 13% -> 24% of each run, Pallas kernels for 0% -> 0%
where the time goes in v1:
time: 208 us
  waiting for transfers between devices  80.7 us (39%)
  blocking collectives  55.6 us (27%)
  local copies, waits for them, and re-layouts  36.4 us (18%)
  matrix products  18.6 us (9%)
  between operations  13.9 us (7%)
  other arithmetic  2.22 us (1%)
    reduce_scatter x1, waiting for transfers between devices, per_device(): lax.psum_scatter(partial_recon.astype(jnp.bfloat16), 'feat', scatter_dime...  47.6 us
    all_gather x2, waiting for transfers between devices, gather_rows(): cols = lax.all_gather(own, 'feat', axis=1, tiled=False)  33.1 us
    psum x1, blocking collectives, per_device(): error_attr = lax.psum(local_terms, 'feat')  28.3 us
    all_to_all x2, blocking collectives, gather_rows(): own = lax.all_to_all(own, 'tok', split_axis=0, concat_axis=0, tiled=True)  27.3 us
    unnamed x21, local copies, waits for them, and re-layouts  19.2 us
    all_gather x2, local copies, waits for them, and re-layouts, gather_rows(): cols = lax.all_gather(own, 'feat', axis=1, tiled=False)  14.8 us
    dot_general x1, matrix products, per_device(): lax.dot_general(rows_g, w_dec, (((0,), (1,)), ((), ())), preferred_elemen...  7.16 us
    dot_general x1, matrix products, per_device(): lax.dot_general(rows_x, w_enc, (((0,), (0,)), ((), ())), preferred_elemen...  6.49 us
  transfers between devices with their start and end apart: 3, of which 3 were waited for; matrix products, arithmetic and copies ran while one was open for 24% of the time, Pallas kernels for 0%

profile of v1, /device:TPU:0, one launch (start us, length us, event | category | flops | bytes accessed | tf_op | source)
XLA Modules:
  0.0 207.6 jit_solution(12167993486928577080)
XLA Ops:
  7.2 0.0 copy-start.3
  7.2 0.0 all-gather.5.cloned.1.call-start
  7.2 1.0 copy.35
  8.3 16.2 %all_to_all.10 = bf16[8,64,256]{2,1,0:T(8,128)(2,1)S(1)} all-to-all(bf16[8,64,256]{2,1,0:T(8,128)(2,1)S(1)} %copy.27), channel_id=1, replica_groups=mesh['tok'=8,'feat'=16] {'tok'}, dimensions={0} | all-to-all | bytes 524288 | tf_op jit(solution)/shard_map/all_to_all | solution.py:14
  24.5 0.9 copy.28
  25.4 0.0 all-gather.5.cloned.1.call-update
  25.4 0.0 all-gather.7.cloned.1.call-start
  25.4 1.0 copy.38
  26.5 11.0 %all_to_all.11 = bf16[8,64,256]{2,1,0:T(8,128)(2,1)S(1)} all-to-all(bf16[8,64,256]{2,1,0:T(8,128)(2,1)S(1)} %copy.32), channel_id=1, replica_groups=mesh['tok'=8,'feat'=16] {'tok'}, dimensions={0} | all-to-all | bytes 524288 | tf_op jit(solution)/shard_map/all_to_all | solution.py:14
  37.6 0.9 copy.33
  38.4 0.0 all-gather.7.cloned.1.call-update
  38.4 0.0 reduce-scatter.2.cloned.1.call-start
  38.5 0.0 copy-done.3
  38.5 0.2 compare_reduce_fusion
  38.7 0.1 copy.30
  38.8 0.2 mul.24
  39.1 0.2 copy.31
  39.3 21.5 %all-gather.5.cloned.1.call-done = bf16[8,1024,256]{2,0,1:T(8,128)(2,1)} async-done(((bf16[8,64,256]{2,0,1:T(8,128)(2,1)}), bf16[8,1024,256]{2,0,1:T(8,128)(2,1)}) %all-gather.5.cloned.1.call-update) | async-done | bytes 4194320 | tf_op jit(solution)/shard_map/all_gather | solution.py:15
  60.8 7.4 %copy.29 = bf16[8,1024,256]{1,0,2:T(8,128)(2,1)} copy(bf16[8,1024,256]{2,0,1:T(8,128)(2,1)} %all-gather.5.cloned.1.call-done) | data formatting | bytes 8388608 | tf_op jit(solution)/shard_map/all_gather | solution.py:15
  68.2 0.0 copy-start.4
  68.2 0.0 slice-start
  68.2 6.7 %copy.36 = bf16[32,8,8,1024]{3,1,2,0:T(8,128)(2,1)S(1)} copy(bf16[32,8,8,1024]{3,2,1,0:T(8,128)(2,1)} %bitcast.38) | data formatting | bytes 8388608
  74.9 0.0 copy-start
  74.9 2.0 copy-done
  76.9 0.0 copy-done.4
  76.9 0.0 slice-start.1
  76.9 0.0 slice-start.2
  76.9 6.5 %fusion.2 = bf16[256,640]{1,0:T(8,128)(2,1)S(1)} fusion(f32[256,640]{1,0:T(8,128)S(1)} %copy.31, bf16[8192,256]{0,1:T(8,128)(2,1)S(1)} %bitcast.40, bf16[8192,640]{1,0:T(8,128)(2,1)} %param.10, f32[640]{0:T(1024)S(1)} %copy-done.4), kind=kOutput, calls=%fused_computation.5 | convolution fusion | flops 2685009920 | bytes 15665664 | tf_op jit(solution)/shard_map/dot_general | solution.py:28
  83.4 0.0 slice-done
  83.4 0.0 slice-done.1
  83.4 0.0 slice-done.2
  83.4 5.0 %convolution_convert_fusion = bf16[256,8192]{1,0:T(8,128)(2,1)} fusion(bf16[256,640]{1,0:T(8,128)(2,1)S(1)} %fusion.2, bf16[640,8192]{1,0:T(8,128)(2,1)S(1)} %bitcast.51), kind=kOutput, calls=%fused_computation | convolution fusion | flops 2686451712 | bytes 15007744 | tf_op jit(solution)/shard_map/dot_general | solution.py:31
  88.4 0.0 reduce-scatter.2.cloned.1.call-update
  88.4 11.6 %all-gather.7.cloned.1.call-done = bf16[8,1024,256]{2,0,1:T(8,128)(2,1)} async-done(((bf16[8,64,256]{2,0,1:T(8,128)(2,1)}), bf16[8,1024,256]{2,0,1:T(8,128)(2,1)}) %all-gather.7.cloned.1.call-update) | async-done | bytes 4194320 | tf_op jit(solution)/shard_map/all_gather | solution.py:15
  100.1 7.4 %copy.34 = bf16[8,1024,256]{1,0,2:T(8,128)(2,1)} copy(bf16[8,1024,256]{2,0,1:T(8,128)(2,1)} %all-gather.7.cloned.1.call-done) | data formatting | bytes 8388608 | tf_op jit(solution)/shard_map/all_gather | solution.py:15
  107.5 6.5 %copy.39 = bf16[32,8,8,1024]{3,1,2,0:T(8,128)(2,1)S(1)} copy(bf16[32,8,8,1024]{3,2,1,0:T(8,128)(2,1)} %bitcast.39) | data formatting | bytes 8388608
  114.0 0.0 copy-start.1
  114.0 1.9 copy-done.1
  115.9 0.0 copy-start.2
  116.0 7.2 %convolution_multiply_fusion = f32[256,640]{1,0:T(8,128)} fusion(bf16[8192,256]{0,1:T(8,128)(2,1)S(1)} %bitcast.42, bf16[640,8192]{1,0:T(8,128)(2,1)} %param.12, bf16[256,640]{1,0:T(8,128)(2,1)S(1)} %fusion.2), kind=kOutput, calls=%fused_computation.1 | convolution fusion | flops 2684682240 | bytes 15663104 | tf_op jit(solution)/shard_map/dot_general | solution.py:43
  123.1 47.6 %reduce-scatter.2.cloned.1.call-done = bf16[256,512]{1,0:T(8,128)(2,1)} async-done(((bf16[256,8192]{1,0:T(8,128)(2,1)}), bf16[256,512]{1,0:T(8,128)(2,1)}) %reduce-scatter.2.cloned.1.call-update) | async-done | bytes 262160 | tf_op jit(solution)/shard_map/reduce_scatter | solution.py:32
  170.7 0.0 copy-done.2
  170.7 2.0 fusion.3
  172.7 28.3 %psum.7 = f32[256]{0:T(256)} all-reduce(f32[256]{0:T(256)S(1)} %get-tuple-element.3), channel_id=1, replica_groups=mesh['tok'=8,'feat'=16] {'feat'}, use_global_device_ids=true, to_apply=%region_3.0 | all-reduce | flops 256 | bytes 2048 | tf_op jit(solution)/shard_map/psum | solution.py:42
  (6 shorter events, 0.2 us)
Async XLA Ops:
  7.2 31.3 %copy-start.3 = (s32[2,20]{1,0:T(2,128)S(1)}, s32[2,20]{1,0:T(2,128)}, u32[]{:S(2)}) copy-start(s32[2,20]{1,0:T(2,128)} %param.9) | copy-start | bytes 484
  7.2 53.6 %all-gather.5.cloned.1.call-start = ((), (), s32[]{:S(2)}) async-start(), calls=%async_computation.4 | async-start | bytes 4456448 | tf_op jit(solution)/shard_map/all_gather | solution.py:15
  25.4 74.7 %all-gather.7.cloned.1.call-start = ((), (), s32[]{:S(2)}) async-start(), calls=%async_computation.5 | async-start | bytes 4456448 | tf_op jit(solution)/shard_map/all_gather | solution.py:15
  38.4 132.3 %reduce-scatter.2.cloned.1.call-start = ((), (), s32[]{:S(2)}) async-start(), calls=%async_computation.3 | async-start | bytes 4456448 | tf_op jit(solution)/shard_map/reduce_scatter | solution.py:32
  68.2 8.7 %copy-start.4 = (f32[640]{0:T(1024)S(1)}, f32[640]{0:T(1024)}, u32[]{:S(2)}) copy-start(f32[640]{0:T(1024)} %param.11) | copy-start | bytes 7684
  68.2 15.2 %slice-start = ((s8[10485760]{0:T(1024)(128)(4,1)}), s8[4194304]{0:T(1024)(128)(4,1)S(1)}, s32[]{:S(2)}) async-start(s8[10485760]{0:T(1024)(128)(4,1)} %bitcast.50), calls=%async_computation.6 | async-start | bytes 8388608
  74.9 2.0 copy-start
  76.9 6.5 %slice-start.1 = ((s8[10485760]{0:T(1024)(128)(4,1)}), s8[4194304]{0:T(1024)(128)(4,1)S(1)}, s32[]{:S(2)}) async-start(s8[10485760]{0:T(1024)(128)(4,1)} %bitcast.50), calls=%async_computation.7 | async-start | bytes 8388608
  76.9 6.5 %slice-start.2 = ((s8[10485760]{0:T(1024)(128)(4,1)}), s8[2097152]{0:T(1024)(128)(4,1)S(1)}, s32[]{:S(2)}) async-start(s8[10485760]{0:T(1024)(128)(4,1)} %bitcast.50), calls=%async_computation.8 | async-start | bytes 4194304
  114.0 1.9 copy-start.1
  115.9 54.8 %copy-start.2 = (f32[512]{0:T(512)S(1)}, f32[512]{0:T(512)}, u32[]{:S(2)}) copy-start(f32[512]{0:T(512)} %param.13) | copy-start | bytes 6148
Sparse Core Ops, SparseCore 0:
  25.5 35.2 all-gather.4
  63.1 36.9 all-gather.6
  102.5 68.1 reduce-scatter.1

commit v2 on v1

v2 whole, which is shorter than its diff:
```python
import functools

import jax
import jax.numpy as jnp
from jax import lax
from jax.experimental import pallas as pl
from jax.experimental.pallas import tpu as pltpu
from jax.sharding import PartitionSpec as P

MESH = pl.DeviceIdType.MESH
F32, BF16 = jnp.float32, jnp.bfloat16
NX, NY = 4, 4
ROWS = 256
FD = 640
NSEM = 220


class Copies:
    def __init__(self, send, recv):
        self.send, self.recv, self.n, self.open = send, recv, 0, []

    def new(self, src, dst, dev):
        k = self.n
        self.n += 1
        return pltpu.make_async_remote_copy(
            src_ref=src, dst_ref=dst, send_sem=self.send.at[k], recv_sem=self.recv.at[k],
            device_id=dev, device_id_type=MESH,
        ), k

    def start(self, src, dst, dev):
        copy, k = self.new(src, dst, dev)
        copy.start()
        self.open.append(copy)
        return k

    def arrived(self, k, mine, dev):
        pltpu.make_async_remote_copy(
            src_ref=mine, dst_ref=mine, send_sem=self.send.at[k], recv_sem=self.recv.at[k],
            device_id=dev, device_id_type=MESH,
        ).wait_recv()

    def drain(self):
        for copy in self.open:
            copy.wait_send()


def kernel(xt, gt, active, wenc_h, benc, wdec_h, bdec, fa_h, err_h, attr_h,
           X, G, wenc, wdec, pre, acts, projt, part, r0, r1, ra, rb, red, reu, rz, errb, fab, sums, got,
           attr, local_sem, send, recv, tsend, trecv):
    tok, feat = lax.axis_index("tok"), lax.axis_index("feat")
    x, zh = tok // 2, tok % 2
    y, z, c = feat // 4, (feat // 2) % 2, feat % 2
    p = feat // 2
    up, dn, opp = (y + 1) % NY, (y + 3) % NY, (y + 2) % NY

    def at(yy, zz, cc):
        return {"tok": tok, "feat": yy * 4 + zz * 2 + cc}

    d_core, d_z, d_up, d_dn = at(y, z, 1 - c), at(y, 1 - z, c), at(up, z, c), at(dn, z, c)

    w1 = pltpu.make_async_copy(wenc_h, wenc, local_sem.at[0])
    w2 = pltpu.make_async_copy(wdec_h, wdec, local_sem.at[1])
    own = []
    for i, (src, dst) in enumerate(((xt, X), (gt, G))):
        own.append(pltpu.make_async_copy(
            src.at[:, pl.ds(pl.multiple_of(tok * ROWS, ROWS), ROWS)], dst.at[p, 0, x, c], local_sem.at[2 + i]))
        own[i].start()
    w1.start()
    w2.start()

    def tok_peer(dx, other):
        xx = (x + dx) % NX
        zz = 1 - zh if other else zh
        return xx * 2 + zz, (y * 2 + (1 - z if other else z)) * 2 + c

    peers = [(dx, o) for o in (0, 1) for dx in range(NX) if dx or o]
    barrier = pltpu.get_barrier_semaphore()
    for dx, o in peers:
        tt, ff = tok_peer(dx, o)
        pl.semaphore_signal(barrier, inc=1, device_id={"tok": tt, "feat": ff}, device_id_type=MESH)
    for dev in (d_core, d_z, d_up, d_dn):
        pl.semaphore_signal(barrier, inc=1, device_id=dev, device_id_type=MESH)
    pl.semaphore_wait(barrier, len(peers) + 4)

    tcopies = []
    for i, (src, dst) in enumerate(((xt, X), (gt, G))):
        for dx, o in ((2, 0), (2, 1), (1, 0), (3, 0), (1, 1), (3, 1), (0, 1)):
            tt, ff = tok_peer(dx, o)
            k = i * 8 + o * 4 + dx
            copy = pltpu.make_async_remote_copy(
                src_ref=src.at[:, pl.ds(pl.multiple_of(tt * ROWS, ROWS), ROWS)],
                dst_ref=dst.at[ff // 2, o, x, c],
                send_sem=tsend.at[k], recv_sem=trecv.at[k],
                device_id={"tok": tt, "feat": ff}, device_id_type=MESH)
            copy.start()
            tcopies.append(copy)

    def tok_arrived(i, dst, o):
        for dx in range(NX):
            if dx or o:
                tt, ff = tok_peer((NX - dx) % NX, o)
                slab = dst.at[p, o, (x + NX - dx) % NX, c]
                k = i * 8 + o * 4 + dx
                pltpu.make_async_remote_copy(
                    src_ref=slab, dst_ref=slab, send_sem=tsend.at[k], recv_sem=trecv.at[k],
                    device_id={"tok": tt, "feat": ff}, device_id_type=MESH).wait_recv()

    cp = Copies(send, recv)

    def blk(buf, yy, zz, s, cc, half=None):
        if half is None:
            return buf.at[yy * 2 + zz, s, :, cc]
        return buf.at[yy * 2 + zz, s, pl.ds(half * 2, 2), cc]

    class Gather:
        def __init__(self, buf):
            self.buf, self.core, self.k = buf, {}, {}

        def send(self, name, yy, zz, s, dev, half=None):
            b = blk(self.buf, yy, zz, s, c, half)
            self.k[name] = cp.start(b, b, dev)

        def wait(self, name, yy, zz, s, dev, half=None):
            cp.arrived(self.k[name], blk(self.buf, yy, zz, s, c, half), dev)

        def to_core(self, name, yy, zz, s):
            b = blk(self.buf, yy, zz, s, c)
            self.core[name] = (cp.start(b, b, d_core), yy, zz, s)

        def from_core(self, name):
            k, yy, zz, s = self.core[name]
            cp.arrived(k, blk(self.buf, yy, zz, s, 1 - c), d_core)

    def gather(buf, step, head):
        g = Gather(buf)
        zo = 1 - z

        def ready(name, yy, zz, s):
            g.from_core(name)
            step(yy, zz, s)

        head(0)
        g.send("z0", y, z, 0, d_z)
        g.send("u0", y, z, 0, d_up)
        g.send("d0", y, z, 0, d_dn)
        g.to_core("o0", y, z, 0)
        head(1)
        g.send("u1", y, z, 1, d_up)
        g.send("d1", y, z, 1, d_dn)
        g.send("z1", y, z, 1, d_z)
        g.to_core("o1", y, z, 1)
        ready("o0", y, z, 0)
        g.wait("z0", y, zo, 0, d_z)
        g.send("uz", y, zo, 0, d_up)
        g.send("dz", y, zo, 0, d_dn)
        g.to_core("p0", y, zo, 0)
        g.wait("u0", dn, z, 0, d_dn)
        g.wait("d0", up, z, 0, d_up)
        g.to_core("u0c", dn, z, 0)
        g.to_core("d0c", up, z, 0)
        ready("o1", y, z, 1)
        ready("p0", y, zo, 0)
        g.wait("u1", dn, z, 1, d_dn)
        g.send("fu1", dn, z, 1, d_up, 0)
        g.send("zu1", dn, z, 1, d_z)
        g.wait("d1", up, z, 1, d_up)
        g.send("fd1", up, z, 1, d_dn, 1)
        g.send("zd1", up, z, 1, d_z)
        g.send("fu0", dn, z, 0, d_up, 0)
        g.send("fd0", up, z, 0, d_dn, 1)
        g.to_core("u1c", dn, z, 1)
        g.to_core("d1c", up, z, 1)
        g.wait("z1", y, zo, 1, d_z)
        g.to_core("p1", y, zo, 1)
        ready("u0c", dn, z, 0)
        ready("d0c", up, z, 0)
        g.wait("uz", dn, zo, 0, d_dn)
        g.send("fuz", dn, zo, 0, d_up, 0)
        g.wait("dz", up, zo, 0, d_up)
        g.send("fdz", up, zo, 0, d_dn, 1)
        g.to_core("uzc", dn, zo, 0)
        g.to_core("dzc", up, zo, 0)
        g.wait("fu1", opp, z, 1, d_dn, 0)
        g.wait("fd1", opp, z, 1, d_up, 1)
        g.send("zo1", opp, z, 1, d_z)
        g.to_core("op1", opp, z, 1)
        ready("u1c", dn, z, 1)
        ready("d1c", up, z, 1)
        ready("p1", y, zo, 1)
        g.wait("zu1", dn, zo, 1, d_z)
        g.to_core("zu1c", dn, zo, 1)
        g.wait("fu0", opp, z, 0, d_dn, 0)
        g.wait("fd0", opp, z, 0, d_up, 1)
        g.to_core("op0", opp, z, 0)
        ready("uzc", dn, zo, 0)
        ready("dzc", up, zo, 0)
        ready("op1", opp, z, 1)
        g.wait("fuz", opp, zo, 0, d_dn, 0)
        g.wait("fdz", opp, zo, 0, d_up, 1)
        g.to_core("opz", opp, zo, 0)
        g.wait("zd1", up, zo, 1, d_z)
        g.to_core("zd1c", up, zo, 1)
        ready("zu1c", dn, zo, 1)
        ready("op0", opp, z, 0)
        ready("opz", opp, zo, 0)
        ready("zd1c", up, zo, 1)
        g.wait("zo1", opp, zo, 1, d_z)
        g.to_core("zo1c", opp, zo, 1)
        ready("zo1c", opp, zo, 1)

    def place(yy, zz, s):
        if s == 0:
            return zh, yy * 2 + zz
        return 1 - zh, yy * 2 + 1 - zz

    pre[...] = jnp.zeros_like(pre)

    def pre_step(yy, zz, s):
        zp, q = place(yy, zz, s)
        lhs = X[yy * 2 + zz, s].reshape(512, ROWS)
        rhs = wenc[:, zp, q].reshape(512, FD)
        pre[...] += lax.dot_general(lhs, rhs, (((0,), (0,)), ((), ())), preferred_element_type=F32)

    def head_x(s):
        if s == 0:
            own[0].wait()
        tok_arrived(0, X, s)
        if s == 1:
            w1.wait()

    gather(X, pre_step, head_x)

    lane_block = feat * 5 + lax.broadcasted_iota(jnp.int32, (1, FD), 1) // 128
    for tile in range(2):
        hit = jnp.zeros((1, FD), F32)
        for j in range(active.shape[1]):
            hit = jnp.where(lane_block == active[tile, j], 1.0, hit)
        rows = pl.ds(tile * 128, 128)
        acts[rows, :] = (jnp.maximum(pre[rows, :] + benc[...].reshape(1, FD), 0.0) * hit).astype(BF16)

    w2.wait()

    @pl.loop(0, 16)
    def _(i):
        q = (i % 8) * 2 + jnp.where(i < 8, 1 - c, c)
        cols = pl.ds(pl.multiple_of(q * 512, 512), 512)
        part[q] = jnp.dot(acts[...], wdec[:, cols], preferred_element_type=F32).astype(BF16)

    core_k = [cp.start(part.at[q * 2 + 1 - c], r0.at[q], d_core) for q in range(8)]

    projt[...] = jnp.zeros_like(projt)

    def proj_step(yy, zz, s):
        zp, q = place(yy, zz, s)
        lhs = jnp.concatenate(
            [wdec[:, pl.ds(pl.multiple_of((xx * 2 + zp) * 1024 + q * 128, 128), 128)] for xx in range(NX)], axis=1)
        projt[...] += jnp.dot(lhs, G[yy * 2 + zz, s].reshape(512, ROWS), preferred_element_type=F32)

    def head_g(s):
        if s == 0:
            own[1].wait()
        tok_arrived(1, G, s)

    gather(G, proj_step, head_g)

    ox, oz = feat // 4, (feat // 2) % 2
    os = jnp.where(oz == zh, 0, 1)
    term = jnp.zeros((ROWS, 128), F32)
    bd = bdec[...].reshape(1, 512)
    for j in range(4):
        q = (feat % 2) * 4 + j
        pb = q + os * (1 - 2 * (q % 2))
        xs = X[pb, os, ox].reshape(128, ROWS).astype(F32).T - bd[:, j * 128:(j + 1) * 128]
        gs = G[pb, os, ox].reshape(128, ROWS).astype(F32).T
        errb[:, j * 128:(j + 1) * 128] = xs
        term = term + xs * gs
    for j in range(5):
        lanes = slice(j * 128, (j + 1) * 128)
        f = acts[:, lanes].astype(F32) * projt[lanes, :].T
        fab[:, lanes] = f
        term = term - f
    out1 = pltpu.make_async_copy(fab, fa_h, local_sem.at[4])
    out1.start()
    sums[0] = jnp.broadcast_to(jnp.sum(term.T, axis=0, keepdims=True), (8, ROWS))

    def pair(i, dev):
        k = cp.start(sums.at[i], got.at[i], dev)
        return lambda: cp.arrived(k, got.at[i], dev)

    def add(dst, *srcs):
        total = dst[...].astype(F32)
        for s in srcs:
            total = total + s[...].astype(F32)
        dst[...] = total.astype(BF16)

    w_pair = pair(0, d_core)
    for q in range(8):
        cp.arrived(core_k[q], r0.at[q], d_core)

    @pl.loop(0, 8)
    def _(q):
        add(part.at[q * 2 + c], r0.at[q])

    def unit(u, yy, lo, n):
        zz = (z, 1 - z, z)[u]
        return part.at[(yy * 2 + zz) * 2 + c, pl.ds((0, 128, 128)[u] + lo, n)]

    zk = [cp.start(part.at[(yy * 2 + 1 - z) * 2 + c, pl.ds(0, 128)], r1.at[yy], d_z) for yy in range(NY)]
    ka, kb, ku, kd = {}, {}, {}, {}

    def first(u):
        ka[u] = cp.start(unit(u, opp, 0, 64), ra.at[u], d_up)
        kb[u] = cp.start(unit(u, opp, 64, 64), rb.at[u], d_dn)

    def second(u):
        cp.arrived(ka[u], ra.at[u], d_dn)
        add(unit(u, up, 0, 64), ra.at[u])
        ku[u] = cp.start(unit(u, up, 0, 128), red.at[u], d_up)
        cp.arrived(kb[u], rb.at[u], d_up)
        add(unit(u, dn, 64, 64), rb.at[u])
        kd[u] = cp.start(unit(u, dn, 0, 128), reu.at[u], d_dn)

    first(1)
    first(2)
    w_pair()
    sums[1] = sums[0] + got[0]
    w_pair = pair(1, d_z)
    second(1)
    for yy in range(NY):
        cp.arrived(zk[yy], r1.at[yy], d_z)

    @pl.loop(0, NY)
    def _(yy):
        add(part.at[(yy * 2 + z) * 2 + c, pl.ds(0, 128)], r1.at[yy])

    first(0)
    w_pair()
    sums[2] = sums[1] + got[1]
    d_even = at(y + 1 - 2 * (y % 2), z, c)
    d_odd = at(3 - y, z, c)
    w_pair = pair(2, d_even)
    second(2)
    cp.arrived(ku[1], red.at[1], d_dn)
    cp.arrived(kd[1], reu.at[1], d_up)
    add(unit(1, y, 0, 128), red.at[1], reu.at[1])
    k_last = cp.start(unit(1, y, 0, 128), rz, d_z)
    w_pair()
    sums[3] = sums[2] + got[2]
    w_pair = pair(3, d_odd)
    second(0)
    w_pair()
    attr[...] = (sums[3] + got[3])[0:1, :]
    out2 = pltpu.make_async_copy(attr, attr_h, local_sem.at[5])
    out2.start()

    cp.arrived(ku[2], red.at[2], d_dn)
    cp.arrived(kd[2], reu.at[2], d_up)
    cp.arrived(k_last, rz, d_z)
    hi = pl.ds(128, 128)
    errb[hi, :] = errb[hi, :] - (unit(2, y, 0, 128)[...].astype(F32) + red[2].astype(F32) + reu[2].astype(F32)
                                 + rz[...].astype(F32))
    out3 = pltpu.make_async_copy(errb.at[hi], err_h.at[hi], local_sem.at[6])
    out3.start()
    cp.arrived(ku[0], red.at[0], d_dn)
    cp.arrived(kd[0], reu.at[0], d_up)
    lo = pl.ds(0, 128)
    errb[lo, :] = errb[lo, :] - (unit(0, y, 0, 128)[...].astype(F32) + red[0].astype(F32) + reu[0].astype(F32))
    out4 = pltpu.make_async_copy(errb.at[lo], err_h.at[lo], local_sem.at[7])
    out4.start()
    for copy in tcopies:
        copy.wait_send()
    cp.drain()
    for o in (out1, out2, out3, out4):
        o.wait()


def per_device(resid, resid_grad, active, w_enc, b_enc, w_dec, b_dec):
    any_, vmem = pl.BlockSpec(memory_space=pl.ANY), pl.BlockSpec(memory_space=pltpu.VMEM)
    V = pltpu.VMEM
    fa, err, attr = pl.pallas_call(
        kernel,
        out_shape=(
            jax.ShapeDtypeStruct((ROWS, FD), F32),
            jax.ShapeDtypeStruct((ROWS, 512), F32),
            jax.ShapeDtypeStruct((1, ROWS), F32),
        ),
        in_specs=[any_, any_, pl.BlockSpec(memory_space=pltpu.SMEM), any_, vmem, any_, vmem],
        out_specs=(any_, any_, any_),
        scratch_shapes=[
            V((8, 2, NX, 2, 64, ROWS), BF16),
            V((8, 2, NX, 2, 64, ROWS), BF16),
            V((NX, 2, 8, 128, FD), BF16),
            V((FD, 8192), BF16),
            V((ROWS, FD), F32),
            V((ROWS, FD), BF16),
            V((FD, ROWS), F32),
            V((16, ROWS, 512), BF16),
            V((8, ROWS, 512), BF16),
            V((NY, 128, 512), BF16),
            V((3, 64, 512), BF16),
            V((3, 64, 512), BF16),
            V((3, 128, 512), BF16),
            V((3, 128, 512), BF16),
            V((128, 512), BF16),
            V((ROWS, 512), F32),
            V((ROWS, FD), F32),
            V((4, 8, ROWS), F32),
            V((4, 8, ROWS), F32),
            V((1, ROWS), F32),
            pltpu.SemaphoreType.DMA((8,)),
            pltpu.SemaphoreType.DMA((NSEM,)),
            pltpu.SemaphoreType.DMA((NSEM,)),
            pltpu.SemaphoreType.DMA((16,)),
            pltpu.SemaphoreType.DMA((16,)),
        ],
        compiler_params=pltpu.CompilerParams(
            collective_id=0, has_side_effects=True, vmem_limit_bytes=60 * 1024 * 1024),
    )(resid.T, resid_grad.T, active, w_enc.reshape(NX, 2, 8, 128, FD), b_enc, w_dec, b_dec)
    return fa, err, attr.reshape(ROWS)


def solution(mesh):
    placed = (
        P(None, ("tok", "feat")),
        P(None, ("tok", "feat")),
        P("tok", None),
        P(None, "feat"),
        P("feat"),
        P("feat", None),
        P("feat"),
    )
    return jax.shard_map(
        per_device,
        mesh=mesh,
        in_specs=placed,
        out_specs=(P("tok", "feat"), P("tok", "feat"), P("tok")),
        check_vma=False,
    )
```

time: 208 us -> 91.1 us (0.44)
  Pallas kernels: 0 us -> 85.1 us
  waiting for transfers between devices: 80.7 us -> 0 us
  blocking collectives: 55.6 us -> 0 us
  local copies, waits for them, and re-layouts: 36.4 us -> 5.05 us
  matrix products: 18.6 us -> 0 us
  between operations: 13.9 us -> 0.64 us
  other arithmetic: 2.22 us -> 0 us
    pallas_call x0 -> x1, Pallas kernels: none -> 85.1 us  [per_device(): pl.pallas_call(kernel, out_shape=(jax.ShapeDtypeStruct((ROWS, FD), F32),...]
    reduce_scatter x1 -> x0, waiting for transfers between devices: 47.6 us -> none  [per_device(): lax.psum_scatter(partial_recon.astype(jnp.bfloat16), 'feat', scatter_dime...]
    all_gather x2 -> x0, waiting for transfers between devices: 33.1 us -> none  [gather_rows(): cols = lax.all_gather(own, 'feat', axis=1, tiled=False)]
    psum x1 -> x0, blocking collectives: 28.3 us -> none  [per_device(): error_attr = lax.psum(local_terms, 'feat')]
    all_to_all x2 -> x0, blocking collectives: 27.3 us -> none  [gather_rows(): own = lax.all_to_all(own, 'tok', split_axis=0, concat_axis=0, tiled=True)]
    dot_general x3 -> x0, matrix products: 18.6 us -> none  [the longest x1 7.16 us: per_device(): lax.dot_general(rows_g, w_dec, (((0,), (1,)), ((), ())), preferred_elemen...]
    all_gather x2 -> x0, local copies, waits for them, and re-layouts: 14.8 us -> none  [gather_rows(): cols = lax.all_gather(own, 'feat', axis=1, tiled=False)]
    unnamed x21 -> x3, local copies, waits for them, and re-layouts: 19.2 us -> 5.05 us
  transfers between devices with their start and end apart: 3 -> 0, of which waited for: 3 -> 0; matrix products, arithmetic and copies ran while one was open for 24% -> 0% of each run, Pallas kernels for 0% -> 0%
where the time goes in v2:
time: 91.1 us; the launch traced here: 90.8 us
  Pallas kernels  85.1 us (93%)
  local copies, waits for them, and re-layouts  5.05 us (6%)
    pallas_call x1, Pallas kernels, per_device(): pl.pallas_call(kernel, out_shape=(jax.ShapeDtypeStruct((ROWS, FD), F32),...  85.1 us
    unnamed x3, local copies, waits for them, and re-layouts  5.05 us

profile of v2, /device:TPU:0, one launch (start us, length us, event | category | flops | bytes accessed | tf_op | source)
XLA Modules:
  0.0 90.8 jit_solution(6721939545593568763)
XLA Ops:
  0.6 85.1 %shard_map.94 = (f32[256,640]{1,0:T(8,128)}, f32[256,512]{1,0:T(8,128)}, f32[1,256]{1,0:T(1,128)}) custom-call(bf16[64,2048]{1,0:T(8,128)(2,1)} %bitcast.5, bf16[64,2048]{1,0:T(8,128)(2,1)} %bitcast.6, s32[2,20]{1,0:T(2,128)} %active.1, bf16[4,2,8,128,640]{4,3,2,1,0:T(8,128)(2,1)} %bitcast.4, f32[640]{0:T(1024)} %benc.1, bf16[640,8192]{1,0:T(8,128)(2,1)} %wdec_h.1, ...), custom_call_target="tpu_custom_call" | custom-call | tf_op jit(solution)/shard_map/pallas_call | solution.py:380
  85.8 2.0 %copy.13 = f32[256,640]{1,0:T(8,128)} copy(f32[256,640]{1,0:T(8,128)} %get-tuple-element.12) | data formatting | bytes 1310720
  87.8 1.9 %copy.14 = f32[256,512]{1,0:T(8,128)} copy(f32[256,512]{1,0:T(8,128)} %get-tuple-element.13) | data formatting | bytes 1048576
  89.6 1.2 %copy.15 = f32[256]{0:T(256)} copy(f32[256]{0:T(256)} %bitcast.7) | data formatting | bytes 2048

commit v3 on v1

v3 whole, which is shorter than its diff:
```python
import contextlib
import math

import jax
import jax.numpy as jnp
from jax import lax
from jax.experimental import pallas as pl
from jax.experimental.pallas import tpu as pltpu
from jax.sharding import PartitionSpec as P

MESH = pl.DeviceIdType.MESH
F32, BF16 = jnp.float32, jnp.bfloat16
NX, NY = 4, 4
ROWS = 256
FD = 640
NRECV = 90
SCOPED = False


def mark(name):
    return jax.named_scope(name) if SCOPED else contextlib.nullcontext()


class Copies:
    def __init__(self, send, recv):
        self.send, self.recv, self.keys, self.sent = send, recv, {}, {}

    def start(self, key, src, dst, dev, group=0):
        k = self.keys.setdefault(key, len(self.keys))
        pltpu.make_async_remote_copy(
            src_ref=src, dst_ref=dst, send_sem=self.send.at[group], recv_sem=self.recv.at[k],
            device_id=dev, device_id_type=MESH,
        ).start()
        self.sent[group] = self.sent.get(group, 0) + math.prod(src.shape) * src.dtype.itemsize

    def arrived(self, key, mine, dev):
        with mark(f"w{key}"):
            pltpu.make_async_remote_copy(
                src_ref=mine, dst_ref=mine, send_sem=self.send.at[0], recv_sem=self.recv.at[self.keys[key]],
                device_id=dev, device_id_type=MESH,
            ).wait_recv()

    def drain(self, group, rows, row_bytes, dev):
        count, rest = divmod(self.sent[group], row_bytes)
        assert rest == 0
        mine = rows(count)
        pltpu.make_async_remote_copy(
            src_ref=mine, dst_ref=mine, send_sem=self.send.at[group], recv_sem=self.recv.at[0],
            device_id=dev, device_id_type=MESH,
        ).wait_send()


def kernel(xt, gt, active, wenc_h, benc, wdec_h, bdec, fab, errb, attr,
           X, G, wenc, wdec, wpeer, pre, acts, apeer, projt, part, r1, ra, rb, red, reu, rz, sums, got,
           local_sem, send, recv):
    tok, feat = lax.axis_index("tok"), lax.axis_index("feat")
    x, zh = tok // 2, tok % 2
    y, z, c = feat // 4, (feat // 2) % 2, feat % 2
    p = feat // 2
    up, dn, opp = (y + 1) % NY, (y + 3) % NY, (y + 2) % NY

    def at(yy, zz, cc):
        return {"tok": tok, "feat": yy * 4 + zz * 2 + cc}

    d_core, d_z, d_up, d_dn = at(y, z, 1 - c), at(y, 1 - z, c), at(up, z, c), at(dn, z, c)

    w1 = pltpu.make_async_copy(wenc_h, wenc, local_sem.at[0])
    w2 = pltpu.make_async_copy(wdec_h, wdec, local_sem.at[1])
    own = []
    for i, (src, dst) in enumerate(((xt, X), (gt, G))):
        own.append(pltpu.make_async_copy(
            src.at[:, pl.ds(pl.multiple_of(tok * ROWS, ROWS), ROWS)], dst.at[p, 0, x, c], local_sem.at[2 + i]))
        own[i].start()
    w1.start()
    w2.start()

    def tok_peer(dx, other):
        xx = (x + dx) % NX
        zz = 1 - zh if other else zh
        return xx * 2 + zz, (y * 2 + (1 - z if other else z)) * 2 + c

    peers = [(dx, o) for o in (0, 1) for dx in range(NX) if dx or o]
    barrier = pltpu.get_barrier_semaphore()
    for dx, o in peers:
        tt, ff = tok_peer(dx, o)
        pl.semaphore_signal(barrier, inc=1, device_id={"tok": tt, "feat": ff}, device_id_type=MESH)
    d_diag, d_opp = at(y, 1 - z, 1 - c), at(opp, z, c)
    group = (d_core, d_z, d_up, d_dn, d_diag, d_opp)
    for dev in group:
        pl.semaphore_signal(barrier, inc=1, device_id=dev, device_id_type=MESH)
    with mark("barrier"):
        pl.semaphore_wait(barrier, len(peers) + len(group))

    cp = Copies(send, recv)
    for i, (src, dst) in enumerate(((xt, X), (gt, G))):
        for dx, o in ((2, 0), (2, 1), (1, 0), (3, 0), (1, 1), (3, 1), (0, 1)):
            tt, ff = tok_peer(dx, o)
            cp.start(f"t{o}{dx}" if i == 0 else "tg",
                     src.at[:, pl.ds(pl.multiple_of(tt * ROWS, ROWS), ROWS)], dst.at[ff // 2, o, x, c],
                     {"tok": tt, "feat": ff}, 1)

    sent_wpeer = []

    def send_wpeer():
        q = len(sent_wpeer)
        sent_wpeer.append(q)
        cols = pl.ds(pl.multiple_of((q * 2 + 1 - c) * 512, 512), 512)
        cp.start(f"wpeer{q // 4}", wdec_h.at[:, cols], wpeer.at[q], d_core)

    def blk(buf, yy, zz, s, cc, part=None):
        if part is None:
            return buf.at[yy * 2 + zz, s, :, cc]
        return buf.at[yy * 2 + zz, s, part, cc]

    zo = 1 - z
    halves = (pl.ds(0, 2), pl.ds(2, 2))

    class Gather:
        def __init__(self, tag, buf, step):
            self.tag, self.buf, self.step, self.core = tag, buf, step, {}
            self.group = 0 if tag == "x" else 4

        def send(self, name, yy, zz, s, dev, part=None):
            b = blk(self.buf, yy, zz, s, c, part)
            cp.start(self.tag + name, b, b, dev, self.group)

        def wait(self, name, yy, zz, s, dev):
            cp.arrived(self.tag + name, blk(self.buf, yy, zz, s, c), dev)

        def to_core(self, name, yy, zz, s, part=None):
            b = blk(self.buf, yy, zz, s, c, part)
            cp.start(self.tag + name + "c", b, b, d_core, self.group)
            self.core[name] = (yy, zz, s)

        def steps(self, *names):
            for name in names:
                yy, zz, s = self.core[name]
                cp.arrived(self.tag + name + "c", blk(self.buf, yy, zz, s, 1 - c), d_core)
                with mark(f"s{self.tag}{name}"):
                    self.step(yy, zz, s)

        def begin(self):
            self.send("u1", y, z, 1, d_up)
            self.send("d1", y, z, 1, d_dn)
            self.send("z0", y, z, 0, d_z)
            self.send("u0", y, z, 0, d_up)
            self.send("d0", y, z, 0, d_dn)
            self.send("z1", y, z, 1, d_z)
            self.to_core("o0", y, z, 0)
            self.to_core("o1", y, z, 1)

        def begin_slab(self, s, xx):
            self.send(f"u{s}", y, z, s, d_up, xx)
            self.send(f"d{s}", y, z, s, d_dn, xx)
            self.send(f"z{s}", y, z, s, d_z, xx)
            self.to_core(f"o{s}", y, z, s, xx)

        def a(self):
            self.wait("u1", dn, z, 1, d_dn)
            self.send("zu1", dn, z, 1, d_z)
            self.send("f1", dn, z, 1, d_up, halves[0])
            self.wait("d1", up, z, 1, d_up)
            self.send("zd1", up, z, 1, d_z)
            self.send("f1", up, z, 1, d_dn, halves[1])

        def b(self):
            self.wait("z0", y, zo, 0, d_z)
            self.send("uz", y, zo, 0, d_up)
            self.send("dz", y, zo, 0, d_dn)
            self.to_core("p0", y, zo, 0)

        def c(self):
            self.wait("u0", dn, z, 0, d_dn)
            self.send("f0", dn, z, 0, d_up, halves[0])
            self.wait("d0", up, z, 0, d_up)
            self.send("f0", up, z, 0, d_dn, halves[1])
            self.to_core("u0c", dn, z, 0)
            self.to_core("d0c", up, z, 0)
            self.to_core("u1c", dn, z, 1)
            self.to_core("d1c", up, z, 1)

        def c1(self):
            self.wait("z1", y, zo, 1, d_z)
            self.to_core("p1", y, zo, 1)

        def d(self):
            self.wait("f1", opp, z, 1, d_dn)
            self.send("zo1", opp, z, 1, d_z)
            self.to_core("op1", opp, z, 1)

        def e(self):
            self.wait("uz", dn, zo, 0, d_dn)
            self.send("fz", dn, zo, 0, d_up, halves[0])
            self.wait("dz", up, zo, 0, d_up)
            self.send("fz", up, zo, 0, d_dn, halves[1])
            self.to_core("uzc", dn, zo, 0)
            self.to_core("dzc", up, zo, 0)

        def f(self):
            self.wait("f0", opp, z, 0, d_dn)
            self.to_core("op0", opp, z, 0)

        def g(self):
            self.wait("zu1", dn, zo, 1, d_z)
            self.to_core("zu1c", dn, zo, 1)
            self.wait("zd1", up, zo, 1, d_z)
            self.to_core("zd1c", up, zo, 1)

        def h(self):
            self.wait("fz", opp, zo, 0, d_dn)
            self.to_core("opz", opp, zo, 0)

        def i(self):
            self.wait("zo1", opp, zo, 1, d_z)
            self.to_core("zo1c", opp, zo, 1)

    def place(yy, zz, s):
        if s == 0:
            return zh, yy * 2 + zz
        return 1 - zh, yy * 2 + 1 - zz

    pre[...] = jnp.zeros_like(pre)
    projt[...] = jnp.zeros_like(projt)

    def pre_step(yy, zz, s):
        zp, q = place(yy, zz, s)
        lhs = X[yy * 2 + zz, s].reshape(512, ROWS)
        rhs = wenc[:, zp, q].reshape(512, FD)
        pre[...] += lax.dot_general(lhs, rhs, (((0,), (0,)), ((), ())), preferred_element_type=F32)

    def proj_step(yy, zz, s):
        zp, q = place(yy, zz, s)
        lhs = jnp.concatenate(
            [wdec[:, pl.ds(pl.multiple_of((xx * 2 + zp) * 1024 + q * 128, 128), 128)] for xx in range(NX)], axis=1)
        projt[...] += jnp.dot(lhs, G[yy * 2 + zz, s].reshape(512, ROWS), preferred_element_type=F32)

    gx = Gather("x", X, pre_step)
    gg = Gather("g", G, proj_step)
    for o, dx in ((0, 0), (0, 1), (0, 3), (1, 0), (1, 1), (1, 3), (0, 2), (1, 2)):
        if dx or o:
            cp.arrived(f"t{o}{dx}", X.at[p, o, (x + NX - dx) % NX, c], d_z)
        else:
            own[0].wait()
        gx.begin_slab(o, (x + NX - dx) % NX)
    send_wpeer()
    gx.a()
    gx.b()
    send_wpeer()
    gx.c()
    send_wpeer()
    with mark("w1"):
        w1.wait()
    gx.steps("o0")
    gx.c1()
    send_wpeer()
    gx.d()
    send_wpeer()
    gx.steps("o1")
    gx.e()
    send_wpeer()
    own[1].wait()
    cp.arrived("tg", G.at[pl.ds(0, 7), 0, 0, 0], d_z)
    gg.begin()
    gx.steps("p0", "u0c", "d0c")
    gx.f()
    send_wpeer()
    gx.steps("u1c", "d1c", "p1")
    gx.g()
    send_wpeer()
    gx.h()
    gx.steps("uzc", "dzc", "op1", "op0", "zu1c", "opz")
    gx.i()
    gx.steps("zd1c", "zo1c")

    with mark("acts"):
        lane_block = feat * 5 + lax.broadcasted_iota(jnp.int32, (1, FD), 1) // 128
        for tile in range(2):
            hit = jnp.zeros((1, FD), F32)
            for j in range(active.shape[1]):
                hit = jnp.where(lane_block == active[tile, j], 1.0, hit)
            rows = pl.ds(tile * 128, 128)
            acts[rows, :] = (jnp.maximum(pre[rows, :] + benc[...].reshape(1, FD), 0.0) * hit).astype(BF16)
    cp.start("acts", acts, apeer, d_core, 2)
    with mark("w2"):
        w2.wait()

    def share(q):
        cols = pl.ds(pl.multiple_of((q * 2 + c) * 512, 512), 512)
        lhs = jnp.concatenate([acts[...], apeer[...]], axis=1)
        rhs = jnp.concatenate([wdec[:, cols], wpeer[q]], axis=0)
        part[q] = jnp.dot(lhs, rhs, preferred_element_type=F32).astype(BF16)

    def add(dst, *srcs):
        total = dst[...].astype(F32)
        for s in srcs:
            total = total + s[...].astype(F32)
        dst[...] = total.astype(BF16)

    def unit(u, yy, lo, n):
        zz = (z, zo, z)[u]
        return part.at[yy * 2 + zz, pl.ds((0, 128, 128)[u] + lo, n)]

    def first(u):
        cp.start(f"a{u}", unit(u, opp, 0, 64), ra.at[u], d_up, 4)
        cp.start(f"b{u}", unit(u, opp, 64, 64), rb.at[u], d_dn, 4)

    def second(u):
        cp.arrived(f"a{u}", ra.at[u], d_dn)
        add(unit(u, up, 0, 64), ra.at[u])
        cp.start(f"u{u}", unit(u, up, 0, 128), red.at[u], d_up, 4)
        cp.arrived(f"b{u}", rb.at[u], d_up)
        add(unit(u, dn, 64, 64), rb.at[u])
        cp.start(f"d{u}", unit(u, dn, 0, 128), reu.at[u], d_dn, 4)

    def third(u):
        cp.arrived(f"u{u}", red.at[u], d_dn)
        cp.arrived(f"d{u}", reu.at[u], d_up)

    rel = (opp, up, dn, y)

    def zsend(i):
        cp.start(f"z{i}", part.at[rel[i] * 2 + zo, pl.ds(0, 128)], r1.at[i], d_z, 4)

    def zadd(i):
        cp.arrived(f"z{i}", r1.at[i], d_z)
        add(part.at[rel[i] * 2 + z, pl.ds(0, 128)], r1.at[i])

    gg.steps("o0")
    gg.a()
    gg.b()
    cp.arrived("acts", apeer, d_core)
    cp.arrived("wpeer0", wpeer.at[pl.ds(0, 4)], d_core)
    cp.arrived("wpeer1", wpeer.at[pl.ds(4, 4)], d_core)
    with mark("share_a"):
        @pl.loop(0, NY)
        def _(i):
            share(((y + 2 + i) % NY) * 2 + zo)
    gg.c()
    gg.d()
    zsend(0)
    first(1)
    with mark("share_b"):
        @pl.loop(0, NY)
        def _(i):
            share(((y + 2 + i) % NY) * 2 + z)
    gg.e()
    first(2)
    for i in range(1, NY):
        zsend(i)
    gg.c1()
    gg.steps("o1", "p0")
    gg.f()
    gg.steps("u0c")
    gg.g()
    gg.h()
    gg.steps("d0c", "u1c")
    second(1)
    gg.steps("d1c", "p1", "uzc", "dzc", "op0", "op1", "zu1c", "zd1c")
    gg.i()
    gg.steps("opz")
    second(2)
    gg.steps("zo1c")
    with mark("err"):
        ox, oz = feat // 4, (feat // 2) % 2
        os = jnp.where(oz == zh, 0, 1)
        term = jnp.zeros((ROWS, 128), F32)
        bd = bdec[...].reshape(1, 512)
        for j in range(4):
            q = (feat % 2) * 4 + j
            pb = q + os * (1 - 2 * (q % 2))
            xs = X[pb, os, ox].reshape(128, ROWS).astype(F32).T - bd[:, j * 128:(j + 1) * 128]
            gs = G[pb, os, ox].reshape(128, ROWS).astype(F32).T
            errb[:, j * 128:(j + 1) * 128] = xs
            term = term + xs * gs
        for j in range(5):
            lanes = slice(j * 128, (j + 1) * 128)
            f = acts[:, lanes].astype(F32) * projt[lanes, :].T
            fab[:, lanes] = f
            term = term - f
        sums[0] = jnp.broadcast_to(jnp.sum(term.T, axis=0, keepdims=True), (8, ROWS))

    def exchange(key, src, slots, mine, devs):
        slots[mine] = src[...]
        for dev in devs:
            cp.start(key, src, slots.at[mine], dev, 3)

    def total(key, slots):
        cp.arrived(key, slots.at[pl.ds(0, 3)], d_z)
        return slots[0] + slots[1] + slots[2] + slots[3]

    exchange("s0", sums.at[0], got.at[0], z * 2 + c, (d_core, d_z, d_diag))
    zadd(0)
    first(0)
    third(1)
    add(unit(1, y, 0, 128), red.at[1], reu.at[1])
    cp.start("last", unit(1, y, 0, 128), rz, d_z, 4)
    sums[1] = total("s0", got.at[0])
    exchange("s1", sums.at[1], got.at[1], y, (d_up, d_dn, d_opp))
    zadd(1)
    zadd(2)
    second(0)
    third(2)
    zadd(3)
    attr[...] = total("s1", got.at[1])[0:1, :]
    third(0)
    lo = pl.ds(0, 128)
    errb[lo, :] = errb[lo, :] - (unit(0, y, 0, 128)[...].astype(F32) + red[0].astype(F32) + reu[0].astype(F32))
    cp.arrived("last", rz, d_z)
    hi = pl.ds(128, 128)
    errb[hi, :] = errb[hi, :] - (unit(2, y, 0, 128)[...].astype(F32) + red[2].astype(F32) + reu[2].astype(F32)
                                 + rz[...].astype(F32))
    with mark("drain"):
        assert len(cp.keys) == NRECV, len(cp.keys)
        cp.drain(0, lambda n: wdec.at[pl.ds(0, n)], 8192 * 2, d_z)
        cp.drain(4, lambda n: wdec.at[pl.ds(0, n)], 8192 * 2, d_z)
        cp.drain(1, lambda n: X.at[pl.ds(0, n), 0, 0], 65536, d_z)
        cp.drain(2, lambda n: acts, ROWS * FD * 2, d_z)
        cp.drain(3, lambda n: part.at[0, pl.ds(0, n)], 1024, d_z)


def per_device(resid, resid_grad, active, w_enc, b_enc, w_dec, b_dec):
    any_, vmem = pl.BlockSpec(memory_space=pl.ANY), pl.BlockSpec(memory_space=pltpu.VMEM)
    V = pltpu.VMEM
    outs = [((ROWS, FD), F32), ((ROWS, 512), F32), ((1, ROWS), F32)]
    held = pl.pallas_call(
        kernel,
        out_shape=tuple(V(*o) for o in outs),
        in_specs=[any_, any_, pl.BlockSpec(memory_space=pltpu.SMEM), any_, vmem, any_, vmem],
        out_specs=(vmem, vmem, vmem),
        scratch_shapes=[
            V((8, 2, NX, 2, 64, ROWS), BF16),
            V((8, 2, NX, 2, 64, ROWS), BF16),
            V((NX, 2, 8, 128, FD), BF16),
            V((FD, 8192), BF16),
            V((8, FD, 512), BF16),
            V((ROWS, FD), F32),
            V((ROWS, FD), BF16),
            V((ROWS, FD), BF16),
            V((FD, ROWS), F32),
            V((8, ROWS, 512), BF16),
            V((NY, 128, 512), BF16),
            V((3, 64, 512), BF16),
            V((3, 64, 512), BF16),
            V((3, 128, 512), BF16),
            V((3, 128, 512), BF16),
            V((128, 512), BF16),
            V((2, 8, ROWS), F32),
            V((2, 4, 8, ROWS), F32),
            pltpu.SemaphoreType.DMA((4,)),
            pltpu.SemaphoreType.DMA((5,)),
            pltpu.SemaphoreType.DMA((NRECV,)),
        ],
        compiler_params=pltpu.CompilerParams(
            collective_id=0, has_side_effects=True, vmem_limit_bytes=58 * 1024 * 1024),
    )(resid.T, resid_grad.T, active, w_enc.reshape(NX, 2, 8, 128, FD), b_enc, w_dec, b_dec)
    fa, err, attr = held
    return fa, err, attr.reshape(ROWS)


def solution(mesh):
    placed = (
        P(None, ("tok", "feat")),
        P(None, ("tok", "feat")),
        P("tok", None),
        P(None, "feat"),
        P("feat"),
        P("feat", None),
        P("feat"),
    )
    return jax.shard_map(
        per_device,
        mesh=mesh,
        in_specs=placed,
        out_specs=(P("tok", "feat"), P("tok", "feat"), P("tok")),
        check_vma=False,
    )
```

time: 208 us -> 66.2 us (0.32)
  waiting for transfers between devices: 80.7 us -> 0 us
  Pallas kernels: 0 us -> 62.7 us
  blocking collectives: 55.6 us -> 0 us
  local copies, waits for them, and re-layouts: 36.4 us -> 2.19 us
  matrix products: 18.6 us -> 0 us
  between operations: 13.9 us -> 0.64 us
  other arithmetic: 2.22 us -> 0 us
    pallas_call x0 -> x1, Pallas kernels: none -> 62.7 us  [per_device(): pl.pallas_call(kernel, out_shape=tuple((V(*o) for o in outs)), in_specs=[...]
    reduce_scatter x1 -> x0, waiting for transfers between devices: 47.6 us -> none  [per_device(): lax.psum_scatter(partial_recon.astype(jnp.bfloat16), 'feat', scatter_dime...]
    all_gather x2 -> x0, waiting for transfers between devices: 33.1 us -> none  [gather_rows(): cols = lax.all_gather(own, 'feat', axis=1, tiled=False)]
    psum x1 -> x0, blocking collectives: 28.3 us -> none  [per_device(): error_attr = lax.psum(local_terms, 'feat')]
    all_to_all x2 -> x0, blocking collectives: 27.3 us -> none  [gather_rows(): own = lax.all_to_all(own, 'tok', split_axis=0, concat_axis=0, tiled=True)]
    dot_general x3 -> x0, matrix products: 18.6 us -> none  [the longest x1 7.16 us: per_device(): lax.dot_general(rows_g, w_dec, (((0,), (1,)), ((), ())), preferred_elemen...]
    unnamed x21 -> x3, local copies, waits for them, and re-layouts: 19.2 us -> 2.19 us
    all_gather x2 -> x0, local copies, waits for them, and re-layouts: 14.8 us -> none  [gather_rows(): cols = lax.all_gather(own, 'feat', axis=1, tiled=False)]
  transfers between devices with their start and end apart: 3 -> 0, of which waited for: 3 -> 0; matrix products, arithmetic and copies ran while one was open for 24% -> 0% of each run, Pallas kernels for 0% -> 0%
where the time goes in v3:
time: 66.2 us; the launch traced here: 65.6 us
  Pallas kernels  62.7 us (95%)
  local copies, waits for them, and re-layouts  2.19 us (3%)
    pallas_call x1, Pallas kernels, per_device(): pl.pallas_call(kernel, out_shape=tuple((V(*o) for o in outs)), in_specs=[...  62.7 us
    unnamed x3, local copies, waits for them, and re-layouts  2.19 us

profile of v3, /device:TPU:0, one launch (start us, length us, event | category | flops | bytes accessed | tf_op | source)
XLA Modules:
  0.0 65.6 jit_solution(7479432440713139569)
XLA Ops:
  0.6 62.7 %shard_map.94 = (f32[256,640]{1,0:T(8,128)S(1)}, f32[256,512]{1,0:T(8,128)S(1)}, f32[1,256]{1,0:T(1,128)S(1)}) custom-call(bf16[64,2048]{1,0:T(8,128)(2,1)} %bitcast.6, bf16[64,2048]{1,0:T(8,128)(2,1)} %bitcast.7, s32[2,20]{1,0:T(2,128)} %active.1, bf16[4,2,8,128,640]{4,3,2,1,0:T(8,128)(2,1)} %bitcast.5, f32[640]{0:T(1024)} %benc.1, ...), custom_call_target="tpu_custom_call" | custom-call | tf_op jit(solution)/shard_map/pallas_call | solution.py:425
  63.4 0.8 %copy.13 = f32[256,640]{1,0:T(8,128)} copy(f32[256,640]{1,0:T(8,128)S(1)} %get-tuple-element.9) | data formatting | bytes 1310720
  64.2 0.6 copy.15
  64.8 0.8 %copy.14 = f32[256,512]{1,0:T(8,128)} copy(f32[256,512]{1,0:T(8,128)S(1)} %get-tuple-element.10) | data formatting | bytes 1048576

commit v4 on v3

--- a/solution.py
+++ b/solution.py
@@ -14,6 +14,7 @@
 ROWS = 256
 FD = 640
 NRECV = 90
+N1, N2 = 96, 160
 SCOPED = False
 
 
@@ -50,7 +51,8 @@
         ).wait_send()
 
 
-def kernel(xt, gt, active, wenc_h, benc, wdec_h, bdec, fab, errb, attr,
+def kernel(xt, gt, active_h, wenc_h, benc_h, wdec_h, bdec_h, fab, errb, attr,
+           active, benc, bdec,
            X, G, wenc, wdec, wpeer, pre, acts, apeer, projt, part, r1, ra, rb, red, reu, rz, sums, got,
            local_sem, send, recv):
     tok, feat = lax.axis_index("tok"), lax.axis_index("feat")
@@ -63,16 +65,6 @@
         return {"tok": tok, "feat": yy * 4 + zz * 2 + cc}
 
     d_core, d_z, d_up, d_dn = at(y, z, 1 - c), at(y, 1 - z, c), at(up, z, c), at(dn, z, c)
-
-    w1 = pltpu.make_async_copy(wenc_h, wenc, local_sem.at[0])
-    w2 = pltpu.make_async_copy(wdec_h, wdec, local_sem.at[1])
-    own = []
-    for i, (src, dst) in enumerate(((xt, X), (gt, G))):
-        own.append(pltpu.make_async_copy(
-            src.at[:, pl.ds(pl.multiple_of(tok * ROWS, ROWS), ROWS)], dst.at[p, 0, x, c], local_sem.at[2 + i]))
-        own[i].start()
-    w1.start()
-    w2.start()
 
     def tok_peer(dx, other):
         xx = (x + dx) % NX
@@ -88,12 +80,26 @@
     group = (d_core, d_z, d_up, d_dn, d_diag, d_opp)
     for dev in group:
         pl.semaphore_signal(barrier, inc=1, device_id=dev, device_id_type=MESH)
+    small = [pltpu.make_async_copy(s, d, local_sem.at[4 + i])
+             for i, (s, d) in enumerate(((active_h, active), (benc_h, benc), (bdec_h, bdec)))]
+    w1 = pltpu.make_async_copy(wenc_h, wenc, local_sem.at[0])
+    w2 = pltpu.make_async_copy(wdec_h, wdec, local_sem.at[1])
+    own = []
+    for i, (src, dst) in enumerate(((xt, X), (gt, G))):
+        own.append(pltpu.make_async_copy(
+            src.at[:, pl.ds(pl.multiple_of(tok * ROWS, ROWS), ROWS)], dst.at[p, 0, x, c], local_sem.at[2 + i]))
+        own[i].start()
+    w1.start()
+    for copy in small:
+        copy.start()
+    w2.start()
+
     with mark("barrier"):
         pl.semaphore_wait(barrier, len(peers) + len(group))
 
     cp = Copies(send, recv)
     for i, (src, dst) in enumerate(((xt, X), (gt, G))):
-        for dx, o in ((2, 0), (2, 1), (1, 0), (3, 0), (1, 1), (3, 1), (0, 1)):
+        for dx, o in ((1, 0), (3, 0), (0, 1), (1, 1), (3, 1), (2, 0), (2, 1)):
             tt, ff = tok_peer(dx, o)
             cp.start(f"t{o}{dx}" if i == 0 else "tg",
                      src.at[:, pl.ds(pl.multiple_of(tt * ROWS, ROWS), ROWS)], dst.at[ff // 2, o, x, c],
@@ -142,11 +148,9 @@
         def begin(self):
             self.send("u1", y, z, 1, d_up)
             self.send("d1", y, z, 1, d_dn)
-            self.send("z0", y, z, 0, d_z)
-            self.send("u0", y, z, 0, d_up)
-            self.send("d0", y, z, 0, d_dn)
+            for dx in (1, 2, 3):
+                self.begin_slab(0, (x + NX - dx) % NX)
             self.send("z1", y, z, 1, d_z)
-            self.to_core("o0", y, z, 0)
             self.to_core("o1", y, z, 1)
 
         def begin_slab(self, s, xx):
@@ -242,35 +246,39 @@
         else:
             own[0].wait()
         gx.begin_slab(o, (x + NX - dx) % NX)
+        if dx == 0 and o == 0:
+            own[1].wait()
+            gg.begin_slab(0, x)
+        if (o, dx) in ((0, 0), (0, 1), (1, 0)):
+            send_wpeer()
     send_wpeer()
     gx.a()
     gx.b()
-    send_wpeer()
     gx.c()
     send_wpeer()
     with mark("w1"):
         w1.wait()
-    gx.steps("o0")
+        for copy in small:
+            copy.wait()
+    gx.steps("o0", "o1")
     gx.c1()
     send_wpeer()
+    gx.steps("p0", "u0c")
     gx.d()
     send_wpeer()
-    gx.steps("o1")
+    gx.steps("d0c", "u1c", "d1c", "p1")
     gx.e()
-    send_wpeer()
-    own[1].wait()
     cp.arrived("tg", G.at[pl.ds(0, 7), 0, 0, 0], d_z)
     gg.begin()
-    gx.steps("p0", "u0c", "d0c")
+    send_wpeer()
     gx.f()
-    send_wpeer()
-    gx.steps("u1c", "d1c", "p1")
     gx.g()
-    send_wpeer()
+    gx.steps("op1", "uzc", "dzc", "op0")
     gx.h()
-    gx.steps("uzc", "dzc", "op1", "op0", "zu1c", "opz")
     gx.i()
-    gx.steps("zd1c", "zo1c")
+    gx.steps("zu1c", "zd1c", "opz")
+    gg.a()
+    gx.steps("zo1c")
 
     with mark("acts"):
         lane_block = feat * 5 + lax.broadcasted_iota(jnp.int32, (1, FD), 1) // 128
@@ -298,36 +306,42 @@
 
     def unit(u, yy, lo, n):
         zz = (z, zo, z)[u]
-        return part.at[yy * 2 + zz, pl.ds((0, 128, 128)[u] + lo, n)]
+        return part.at[yy * 2 + zz, pl.ds((0, N1, N1)[u] + lo, n)]
+
+    rows_of, cut = (N1, N2, N2), (48, 80, 80)
+
+    def land(buf, u, n):
+        return buf.at[u, pl.ds(0, n)]
 
     def first(u):
-        cp.start(f"a{u}", unit(u, opp, 0, 64), ra.at[u], d_up, 4)
-        cp.start(f"b{u}", unit(u, opp, 64, 64), rb.at[u], d_dn, 4)
+        a, b = cut[u], rows_of[u] - cut[u]
+        cp.start(f"a{u}", unit(u, opp, 0, a), land(ra, u, a), d_up, 4)
+        cp.start(f"b{u}", unit(u, opp, a, b), land(rb, u, b), d_dn, 4)
 
     def second(u):
-        cp.arrived(f"a{u}", ra.at[u], d_dn)
-        add(unit(u, up, 0, 64), ra.at[u])
-        cp.start(f"u{u}", unit(u, up, 0, 128), red.at[u], d_up, 4)
-        cp.arrived(f"b{u}", rb.at[u], d_up)
-        add(unit(u, dn, 64, 64), rb.at[u])
-        cp.start(f"d{u}", unit(u, dn, 0, 128), reu.at[u], d_dn, 4)
+        n, a, b = rows_of[u], cut[u], rows_of[u] - cut[u]
+        cp.arrived(f"a{u}", land(ra, u, a), d_dn)
+        add(unit(u, up, 0, a), land(ra, u, a))
+        cp.start(f"u{u}", unit(u, up, 0, n), land(red, u, n), d_up, 4)
+        cp.arrived(f"b{u}", land(rb, u, b), d_up)
+        add(unit(u, dn, a, b), land(rb, u, b))
+        cp.start(f"d{u}", unit(u, dn, 0, n), land(reu, u, n), d_dn, 4)
 
     def third(u):
-        cp.arrived(f"u{u}", red.at[u], d_dn)
-        cp.arrived(f"d{u}", reu.at[u], d_up)
+        cp.arrived(f"u{u}", land(red, u, rows_of[u]), d_dn)
+        cp.arrived(f"d{u}", land(reu, u, rows_of[u]), d_up)
 
     rel = (opp, up, dn, y)
 
     def zsend(i):
-        cp.start(f"z{i}", part.at[rel[i] * 2 + zo, pl.ds(0, 128)], r1.at[i], d_z, 4)
+        cp.start(f"z{i}", part.at[rel[i] * 2 + zo, pl.ds(0, N1)], r1.at[i], d_z, 4)
 
     def zadd(i):
         cp.arrived(f"z{i}", r1.at[i], d_z)
-        add(part.at[rel[i] * 2 + z, pl.ds(0, 128)], r1.at[i])
-
-    gg.steps("o0")
-    gg.a()
+        add(part.at[rel[i] * 2 + z, pl.ds(0, N1)], r1.at[i])
+
     gg.b()
+    gg.steps("o0", "o1")
     cp.arrived("acts", apeer, d_core)
     cp.arrived("wpeer0", wpeer.at[pl.ds(0, 4)], d_core)
     cp.arrived("wpeer1", wpeer.at[pl.ds(4, 4)], d_core)
@@ -337,27 +351,27 @@
             share(((y + 2 + i) % NY) * 2 + zo)
     gg.c()
     gg.d()
-    zsend(0)
     first(1)
+    gg.c1()
     with mark("share_b"):
         @pl.loop(0, NY)
         def _(i):
             share(((y + 2 + i) % NY) * 2 + z)
     gg.e()
+    zsend(0)
+    zsend(1)
     first(2)
-    for i in range(1, NY):
-        zsend(i)
-    gg.c1()
-    gg.steps("o1", "p0")
+    gg.steps("p0", "u0c")
     gg.f()
-    gg.steps("u0c")
-    gg.g()
-    gg.h()
     gg.steps("d0c", "u1c")
     second(1)
-    gg.steps("d1c", "p1", "uzc", "dzc", "op0", "op1", "zu1c", "zd1c")
+    gg.g()
+    gg.steps("d1c", "p1")
+    gg.h()
+    gg.steps("uzc", "dzc", "op0", "op1")
     gg.i()
-    gg.steps("opz")
+    zsend(2)
+    gg.steps("zu1c", "zd1c", "opz")
     second(2)
     gg.steps("zo1c")
     with mark("err"):
@@ -389,25 +403,25 @@
         return slots[0] + slots[1] + slots[2] + slots[3]
 
     exchange("s0", sums.at[0], got.at[0], z * 2 + c, (d_core, d_z, d_diag))
+    zsend(3)
     zadd(0)
     first(0)
     third(1)
-    add(unit(1, y, 0, 128), red.at[1], reu.at[1])
-    cp.start("last", unit(1, y, 0, 128), rz, d_z, 4)
+    add(unit(1, y, 0, N2), red.at[1], reu.at[1])
+    cp.start("last", unit(1, y, 0, N2), rz, d_z, 4)
+    zadd(1)
     sums[1] = total("s0", got.at[0])
     exchange("s1", sums.at[1], got.at[1], y, (d_up, d_dn, d_opp))
-    zadd(1)
     zadd(2)
     second(0)
     third(2)
     zadd(3)
     attr[...] = total("s1", got.at[1])[0:1, :]
     third(0)
-    lo = pl.ds(0, 128)
-    errb[lo, :] = errb[lo, :] - (unit(0, y, 0, 128)[...].astype(F32) + red[0].astype(F32) + reu[0].astype(F32))
+    lo, hi = pl.ds(0, N1), pl.ds(N1, N2)
+    errb[lo, :] = errb[lo, :] - (unit(0, y, 0, N1)[...].astype(F32) + red[0, lo].astype(F32) + reu[0, lo].astype(F32))
     cp.arrived("last", rz, d_z)
-    hi = pl.ds(128, 128)
-    errb[hi, :] = errb[hi, :] - (unit(2, y, 0, 128)[...].astype(F32) + red[2].astype(F32) + reu[2].astype(F32)
+    errb[hi, :] = errb[hi, :] - (unit(2, y, 0, N2)[...].astype(F32) + red[2].astype(F32) + reu[2].astype(F32)
                                  + rz[...].astype(F32))
     with mark("drain"):
         assert len(cp.keys) == NRECV, len(cp.keys)
@@ -418,6 +432,15 @@
         cp.drain(3, lambda n: part.at[0, pl.ds(0, n)], 1024, d_z)
 
 
+def write_out(fa, err, attr, fa_h, err_h, attr_h, sem):
+    copies = [pltpu.make_async_copy(s, d, sem.at[i])
+              for i, (s, d) in enumerate(((fa, fa_h), (err, err_h), (attr, attr_h)))]
+    for copy in copies:
+        copy.start()
+    for copy in copies:
+        copy.wait()
+
+
 def per_device(resid, resid_grad, active, w_enc, b_enc, w_dec, b_dec):
     any_, vmem = pl.BlockSpec(memory_space=pl.ANY), pl.BlockSpec(memory_space=pltpu.VMEM)
     V = pltpu.VMEM
@@ -425,9 +448,12 @@
     held = pl.pallas_call(
         kernel,
         out_shape=tuple(V(*o) for o in outs),
-        in_specs=[any_, any_, pl.BlockSpec(memory_space=pltpu.SMEM), any_, vmem, any_, vmem],
+        in_specs=[any_] * 7,
         out_specs=(vmem, vmem, vmem),
         scratch_shapes=[
+            pltpu.SMEM(active.shape, active.dtype),
+            V(b_enc.shape, F32),
+            V(b_dec.shape, F32),
             V((8, 2, NX, 2, 64, ROWS), BF16),
             V((8, 2, NX, 2, 64, ROWS), BF16),
             V((NX, 2, 8, 128, FD), BF16),
@@ -438,22 +464,28 @@
             V((ROWS, FD), BF16),
             V((FD, ROWS), F32),
             V((8, ROWS, 512), BF16),
-            V((NY, 128, 512), BF16),
-            V((3, 64, 512), BF16),
-            V((3, 64, 512), BF16),
-            V((3, 128, 512), BF16),
-            V((3, 128, 512), BF16),
-            V((128, 512), BF16),
+            V((NY, N1, 512), BF16),
+            V((3, 80, 512), BF16),
+            V((3, 80, 512), BF16),
+            V((3, N2, 512), BF16),
+            V((3, N2, 512), BF16),
+            V((N2, 512), BF16),
             V((2, 8, ROWS), F32),
             V((2, 4, 8, ROWS), F32),
-            pltpu.SemaphoreType.DMA((4,)),
+            pltpu.SemaphoreType.DMA((7,)),
             pltpu.SemaphoreType.DMA((5,)),
             pltpu.SemaphoreType.DMA((NRECV,)),
         ],
         compiler_params=pltpu.CompilerParams(
             collective_id=0, has_side_effects=True, vmem_limit_bytes=58 * 1024 * 1024),
     )(resid.T, resid_grad.T, active, w_enc.reshape(NX, 2, 8, 128, FD), b_enc, w_dec, b_dec)
-    fa, err, attr = held
+    fa, err, attr = pl.pallas_call(
+        write_out,
+        out_shape=tuple(jax.ShapeDtypeStruct(*o) for o in outs),
+        in_specs=[vmem] * 3,
+        out_specs=(any_,) * 3,
+        scratch_shapes=[pltpu.SemaphoreType.DMA((3,))],
+    )(*(pltpu.with_memory_space_constraint(h, pltpu.VMEM) for h in held))
     return fa, err, attr.reshape(ROWS)
 
 

time: 66.2 us -> 57.3 us (0.87)
  Pallas kernels: 62.7 us -> 56.5 us
  local copies, waits for them, and re-layouts: 2.19 us -> 0 us
    pallas_call x1, Pallas kernels: 62.7 us -> 55.5 us  [per_device(): pl.pallas_call(kernel, out_shape=tuple((V(*o) for o in outs)), in_specs=[...]
    unnamed x3 -> x0, local copies, waits for them, and re-layouts: 2.19 us -> none
    pallas_call x0 -> x1, Pallas kernels: none -> 1.04 us  [per_device(): pl.pallas_call(write_out, out_shape=tuple((jax.ShapeDtypeStruct(*o) for o...]
where the time goes in v4:
time: 57.3 us; the launch traced here: 57.2 us
  Pallas kernels  56.5 us (99%)
  between operations  0.64 us (1%)
    pallas_call x1, Pallas kernels, per_device(): pl.pallas_call(kernel, out_shape=tuple((V(*o) for o in outs)), in_specs=[...  55.5 us

profile of v4, /device:TPU:0, one launch (start us, length us, event | category | flops | bytes accessed | tf_op | source)
XLA Modules:
  0.0 57.2 jit_solution(10282286395667145260)
XLA Ops:
  0.6 55.5 %shard_map.94 = (f32[256,640]{1,0:T(8,128)S(1)}, f32[256,512]{1,0:T(8,128)S(1)}, f32[1,256]{1,0:T(1,128)S(1)}) custom-call(bf16[64,2048]{1,0:T(8,128)(2,1)} %bitcast.5, bf16[64,2048]{1,0:T(8,128)(2,1)} %bitcast.6, s32[2,20]{1,0:T(2,128)} %active_h.1, bf16[4,2,8,128,640]{4,3,2,1,0:T(8,128)(2,1)} %bitcast.4, f32[640]{0:T(1024)} %benc_h.1, ...), custom_call_target="tpu_custom_call" | custom-call | tf_op jit(solution)/shard_map/pallas_call | solution.py:448
  56.1 1.0 %shard_map.95 = (f32[256,640]{1,0:T(8,128)}, f32[256,512]{1,0:T(8,128)}, f32[1,256]{1,0:T(1,128)}) custom-call(f32[256,640]{1,0:T(8,128)S(1)} %get-tuple-element.9.fa, f32[256,512]{1,0:T(8,128)S(1)} %get-tuple-element.10.err, f32[1,256]{1,0:T(1,128)S(1)} %get-tuple-element.11.attr), custom_call_target="tpu_custom_call" | custom-call | tf_op jit(solution)/shard_map/pallas_call | solution.py:482

commit v5 on v4

--- a/solution.py
+++ b/solution.py
@@ -13,7 +13,7 @@
 NX, NY = 4, 4
 ROWS = 256
 FD = 640
-NRECV = 90
+NRECV = 92
 N1, N2 = 96, 160
 SCOPED = False
 
@@ -101,7 +101,7 @@
     for i, (src, dst) in enumerate(((xt, X), (gt, G))):
         for dx, o in ((1, 0), (3, 0), (0, 1), (1, 1), (3, 1), (2, 0), (2, 1)):
             tt, ff = tok_peer(dx, o)
-            cp.start(f"t{o}{dx}" if i == 0 else "tg",
+            cp.start(f"t{o}{dx}" if i == 0 else f"tg{dx}" if o == 0 and dx != 2 else "tg",
                      src.at[:, pl.ds(pl.multiple_of(tt * ROWS, ROWS), ROWS)], dst.at[ff // 2, o, x, c],
                      {"tok": tt, "feat": ff}, 1)
 
@@ -148,8 +148,7 @@
         def begin(self):
             self.send("u1", y, z, 1, d_up)
             self.send("d1", y, z, 1, d_dn)
-            for dx in (1, 2, 3):
-                self.begin_slab(0, (x + NX - dx) % NX)
+            self.begin_slab(0, (x + 2) % NX)
             self.send("z1", y, z, 1, d_z)
             self.to_core("o1", y, z, 1)
 
@@ -251,6 +250,10 @@
             gg.begin_slab(0, x)
         if (o, dx) in ((0, 0), (0, 1), (1, 0)):
             send_wpeer()
+    for dx in (1, 3):
+        xx = (x + NX - dx) % NX
+        cp.arrived(f"tg{dx}", G.at[p, 0, xx, c], d_z)
+        gg.begin_slab(0, xx)
     send_wpeer()
     gx.a()
     gx.b()
@@ -266,19 +269,22 @@
     gx.steps("p0", "u0c")
     gx.d()
     send_wpeer()
-    gx.steps("d0c", "u1c", "d1c", "p1")
+    gx.steps("d0c")
     gx.e()
-    cp.arrived("tg", G.at[pl.ds(0, 7), 0, 0, 0], d_z)
+    cp.arrived("tg", G.at[pl.ds(0, 5), 0, 0, 0], d_z)
     gg.begin()
     send_wpeer()
+    gx.steps("u1c", "d1c", "p1")
     gx.f()
     gx.g()
     gx.steps("op1", "uzc", "dzc", "op0")
     gx.h()
     gx.i()
-    gx.steps("zu1c", "zd1c", "opz")
     gg.a()
-    gx.steps("zo1c")
+    gx.steps("zu1c", "zd1c")
+    gg.b()
+    gg.c()
+    gx.steps("opz", "zo1c")
 
     with mark("acts"):
         lane_block = feat * 5 + lax.broadcasted_iota(jnp.int32, (1, FD), 1) // 128
@@ -340,40 +346,43 @@
         cp.arrived(f"z{i}", r1.at[i], d_z)
         add(part.at[rel[i] * 2 + z, pl.ds(0, N1)], r1.at[i])
 
-    gg.b()
-    gg.steps("o0", "o1")
+    gg.steps("o0")
+    gg.d()
     cp.arrived("acts", apeer, d_core)
     cp.arrived("wpeer0", wpeer.at[pl.ds(0, 4)], d_core)
     cp.arrived("wpeer1", wpeer.at[pl.ds(4, 4)], d_core)
-    with mark("share_a"):
-        @pl.loop(0, NY)
-        def _(i):
-            share(((y + 2 + i) % NY) * 2 + zo)
-    gg.c()
-    gg.d()
+
+    def shares(name, lo, n):
+        with mark(name):
+            @pl.loop(lo, lo + n)
+            def _(i):
+                k = i // 2
+                yy = (y + k + k // 2) % NY if lo else opp
+                share(yy * 2 + jnp.where(i % 2 == 0, zo, z))
+
+    shares("share0", 0, 2)
     first(1)
+    first(2)
+    zsend(0)
+    shares("share1", 2, 4)
+    zsend(1)
+    zsend(2)
+    gg.e()
     gg.c1()
-    with mark("share_b"):
-        @pl.loop(0, NY)
-        def _(i):
-            share(((y + 2 + i) % NY) * 2 + z)
-    gg.e()
-    zsend(0)
-    zsend(1)
-    first(2)
-    gg.steps("p0", "u0c")
     gg.f()
-    gg.steps("d0c", "u1c")
+    gg.g()
+    shares("share2", 6, 2)
+    zsend(3)
+    gg.steps("o1", "p0")
     second(1)
-    gg.g()
-    gg.steps("d1c", "p1")
+    gg.i()
+    gg.steps("u0c", "d0c", "u1c", "d1c", "p1")
+    zadd(0)
+    first(0)
+    second(2)
+    gg.steps("uzc", "dzc", "op1")
     gg.h()
-    gg.steps("uzc", "dzc", "op0", "op1")
-    gg.i()
-    zsend(2)
-    gg.steps("zu1c", "zd1c", "opz")
-    second(2)
-    gg.steps("zo1c")
+    gg.steps("op0", "zu1c", "zd1c", "zo1c", "opz")
     with mark("err"):
         ox, oz = feat // 4, (feat // 2) % 2
         os = jnp.where(oz == zh, 0, 1)
@@ -403,26 +412,24 @@
         return slots[0] + slots[1] + slots[2] + slots[3]
 
     exchange("s0", sums.at[0], got.at[0], z * 2 + c, (d_core, d_z, d_diag))
-    zsend(3)
-    zadd(0)
-    first(0)
     third(1)
     add(unit(1, y, 0, N2), red.at[1], reu.at[1])
     cp.start("last", unit(1, y, 0, N2), rz, d_z, 4)
     zadd(1)
+    zadd(2)
+    second(0)
     sums[1] = total("s0", got.at[0])
     exchange("s1", sums.at[1], got.at[1], y, (d_up, d_dn, d_opp))
-    zadd(2)
-    second(0)
+    zadd(3)
     third(2)
-    zadd(3)
+    hi = pl.ds(N1, N2)
+    errb[hi, :] = errb[hi, :] - (unit(2, y, 0, N2)[...].astype(F32) + red[2].astype(F32) + reu[2].astype(F32))
+    cp.arrived("last", rz, d_z)
+    errb[hi, :] = errb[hi, :] - rz[...].astype(F32)
+    third(0)
+    lo = pl.ds(0, N1)
+    errb[lo, :] = errb[lo, :] - (unit(0, y, 0, N1)[...].astype(F32) + red[0, lo].astype(F32) + reu[0, lo].astype(F32))
     attr[...] = total("s1", got.at[1])[0:1, :]
-    third(0)
-    lo, hi = pl.ds(0, N1), pl.ds(N1, N2)
-    errb[lo, :] = errb[lo, :] - (unit(0, y, 0, N1)[...].astype(F32) + red[0, lo].astype(F32) + reu[0, lo].astype(F32))
-    cp.arrived("last", rz, d_z)
-    errb[hi, :] = errb[hi, :] - (unit(2, y, 0, N2)[...].astype(F32) + red[2].astype(F32) + reu[2].astype(F32)
-                                 + rz[...].astype(F32))
     with mark("drain"):
         assert len(cp.keys) == NRECV, len(cp.keys)
         cp.drain(0, lambda n: wdec.at[pl.ds(0, n)], 8192 * 2, d_z)

time: 57.3 us -> 55.7 us (0.972)
  Pallas kernels: 56.5 us -> 55 us
    pallas_call x1, Pallas kernels: 55.5 us -> 53.9 us  [per_device(): pl.pallas_call(kernel, out_shape=tuple((V(*o) for o in outs)), in_specs=[...]
where the time goes in v5:
time: 55.7 us; the launch traced here: 55.6 us
  Pallas kernels  55 us (99%)
  between operations  0.64 us (1%)
    pallas_call x1, Pallas kernels, per_device(): pl.pallas_call(kernel, out_shape=tuple((V(*o) for o in outs)), in_specs=[...  53.9 us

profile of v5, /device:TPU:0, one launch (start us, length us, event | category | flops | bytes accessed | tf_op | source)
XLA Modules:
  0.0 55.6 jit_solution(10059289686144193113)
XLA Ops:
  0.6 53.9 %shard_map.94 = (f32[256,640]{1,0:T(8,128)S(1)}, f32[256,512]{1,0:T(8,128)S(1)}, f32[1,256]{1,0:T(1,128)S(1)}) custom-call(bf16[64,2048]{1,0:T(8,128)(2,1)} %bitcast.5, bf16[64,2048]{1,0:T(8,128)(2,1)} %bitcast.6, s32[2,20]{1,0:T(2,128)} %active_h.1, bf16[4,2,8,128,640]{4,3,2,1,0:T(8,128)(2,1)} %bitcast.4, f32[640]{0:T(1024)} %benc_h.1, ...), custom_call_target="tpu_custom_call" | custom-call | tf_op jit(solution)/shard_map/pallas_call | solution.py:455
  54.6 1.0 %shard_map.95 = (f32[256,640]{1,0:T(8,128)}, f32[256,512]{1,0:T(8,128)}, f32[1,256]{1,0:T(1,128)}) custom-call(f32[256,640]{1,0:T(8,128)S(1)} %get-tuple-element.9.fa, f32[256,512]{1,0:T(8,128)S(1)} %get-tuple-element.10.err, f32[1,256]{1,0:T(1,128)S(1)} %get-tuple-element.11.attr), custom_call_target="tpu_custom_call" | custom-call | tf_op jit(solution)/shard_map/pallas_call | solution.py:489

commit v6 on v5

--- a/solution.py
+++ b/solution.py
@@ -248,27 +248,25 @@
         if dx == 0 and o == 0:
             own[1].wait()
             gg.begin_slab(0, x)
-        if (o, dx) in ((0, 0), (0, 1), (1, 0)):
+        if (o, dx) in ((0, 0), (0, 1), (1, 0), (1, 1)):
             send_wpeer()
     for dx in (1, 3):
         xx = (x + NX - dx) % NX
         cp.arrived(f"tg{dx}", G.at[p, 0, xx, c], d_z)
         gg.begin_slab(0, xx)
     send_wpeer()
+    send_wpeer()
     gx.a()
     gx.b()
     gx.c()
-    send_wpeer()
     with mark("w1"):
         w1.wait()
         for copy in small:
             copy.wait()
     gx.steps("o0", "o1")
     gx.c1()
-    send_wpeer()
     gx.steps("p0", "u0c")
     gx.d()
-    send_wpeer()
     gx.steps("d0c")
     gx.e()
     cp.arrived("tg", G.at[pl.ds(0, 5), 0, 0, 0], d_z)
@@ -277,12 +275,13 @@
     gx.steps("u1c", "d1c", "p1")
     gx.f()
     gx.g()
+    send_wpeer()
     gx.steps("op1", "uzc", "dzc", "op0")
     gx.h()
     gx.i()
+    gg.b()
     gg.a()
     gx.steps("zu1c", "zd1c")
-    gg.b()
     gg.c()
     gx.steps("opz", "zo1c")
 
@@ -347,7 +346,6 @@
         add(part.at[rel[i] * 2 + z, pl.ds(0, N1)], r1.at[i])
 
     gg.steps("o0")
-    gg.d()
     cp.arrived("acts", apeer, d_core)
     cp.arrived("wpeer0", wpeer.at[pl.ds(0, 4)], d_core)
     cp.arrived("wpeer1", wpeer.at[pl.ds(4, 4)], d_core)
@@ -363,6 +361,7 @@
     shares("share0", 0, 2)
     first(1)
     first(2)
+    gg.d()
     zsend(0)
     shares("share1", 2, 4)
     zsend(1)
@@ -440,8 +439,9 @@
 
 
 def write_out(fa, err, attr, fa_h, err_h, attr_h, sem):
-    copies = [pltpu.make_async_copy(s, d, sem.at[i])
-              for i, (s, d) in enumerate(((fa, fa_h), (err, err_h), (attr, attr_h)))]
+    cuts = [pl.ds(i * 64, 64) for i in range(ROWS // 64)]
+    pairs = [(s.at[r], d.at[r]) for s, d in ((fa, fa_h), (err, err_h)) for r in cuts] + [(attr, attr_h)]
+    copies = [pltpu.make_async_copy(s, d, sem.at[i]) for i, (s, d) in enumerate(pairs)]
     for copy in copies:
         copy.start()
     for copy in copies:
@@ -491,7 +491,7 @@
         out_shape=tuple(jax.ShapeDtypeStruct(*o) for o in outs),
         in_specs=[vmem] * 3,
         out_specs=(any_,) * 3,
-        scratch_shapes=[pltpu.SemaphoreType.DMA((3,))],
+        scratch_shapes=[pltpu.SemaphoreType.DMA((9,))],
     )(*(pltpu.with_memory_space_constraint(h, pltpu.VMEM) for h in held))
     return fa, err, attr.reshape(ROWS)
 

time: 55.7 us -> 56 us (level)
  no operation moved by 1% of the time
where the time goes in v6:
time: 56 us; the launch traced here: 55.6 us
  Pallas kernels  55 us (98%)
  between operations  0.64 us (1%)
    pallas_call x1, Pallas kernels, per_device(): pl.pallas_call(kernel, out_shape=tuple((V(*o) for o in outs)), in_specs=[...  53.9 us

profile of v6, /device:TPU:0, one launch (start us, length us, event | category | flops | bytes accessed | tf_op | source)
XLA Modules:
  0.0 55.6 jit_solution(11229939236638839998)
XLA Ops:
  0.6 53.9 %shard_map.94 = (f32[256,640]{1,0:T(8,128)S(1)}, f32[256,512]{1,0:T(8,128)S(1)}, f32[1,256]{1,0:T(1,128)S(1)}) custom-call(bf16[64,2048]{1,0:T(8,128)(2,1)} %bitcast.5, bf16[64,2048]{1,0:T(8,128)(2,1)} %bitcast.6, s32[2,20]{1,0:T(2,128)} %active_h.1, bf16[4,2,8,128,640]{4,3,2,1,0:T(8,128)(2,1)} %bitcast.4, f32[640]{0:T(1024)} %benc_h.1, ...), custom_call_target="tpu_custom_call" | custom-call | tf_op jit(solution)/shard_map/pallas_call | solution.py:455
  54.5 1.1 %shard_map.95 = (f32[256,640]{1,0:T(8,128)}, f32[256,512]{1,0:T(8,128)}, f32[1,256]{1,0:T(1,128)}) custom-call(f32[256,640]{1,0:T(8,128)S(1)} %get-tuple-element.9.fa, f32[256,512]{1,0:T(8,128)S(1)} %get-tuple-element.10.err, f32[1,256]{1,0:T(1,128)S(1)} %get-tuple-element.11.attr), custom_call_target="tpu_custom_call" | custom-call | tf_op jit(solution)/shard_map/pallas_call | solution.py:489

commit v7 on v5

--- a/solution.py
+++ b/solution.py
@@ -13,7 +13,7 @@
 NX, NY = 4, 4
 ROWS = 256
 FD = 640
-NRECV = 92
+NRECV = 88
 N1, N2 = 96, 160
 SCOPED = False
 
@@ -111,7 +111,7 @@
         q = len(sent_wpeer)
         sent_wpeer.append(q)
         cols = pl.ds(pl.multiple_of((q * 2 + 1 - c) * 512, 512), 512)
-        cp.start(f"wpeer{q // 4}", wdec_h.at[:, cols], wpeer.at[q], d_core)
+        cp.start("wpeer", wdec_h.at[:, cols], wpeer.at[q], d_core)
 
     def blk(buf, yy, zz, s, cc, part=None):
         if part is None:
@@ -328,14 +328,13 @@
         n, a, b = rows_of[u], cut[u], rows_of[u] - cut[u]
         cp.arrived(f"a{u}", land(ra, u, a), d_dn)
         add(unit(u, up, 0, a), land(ra, u, a))
-        cp.start(f"u{u}", unit(u, up, 0, n), land(red, u, n), d_up, 4)
+        cp.start(f"e{u}", unit(u, up, 0, n), land(red, u, n), d_up, 4)
         cp.arrived(f"b{u}", land(rb, u, b), d_up)
         add(unit(u, dn, a, b), land(rb, u, b))
-        cp.start(f"d{u}", unit(u, dn, 0, n), land(reu, u, n), d_dn, 4)
+        cp.start(f"e{u}", unit(u, dn, 0, n), land(reu, u, n), d_dn, 4)
 
     def third(u):
-        cp.arrived(f"u{u}", land(red, u, rows_of[u]), d_dn)
-        cp.arrived(f"d{u}", land(reu, u, rows_of[u]), d_up)
+        cp.arrived(f"e{u}", part.at[pl.ds(0, 2), pl.ds(0, rows_of[u])], d_dn)
 
     rel = (opp, up, dn, y)
 
@@ -348,9 +347,16 @@
 
     gg.steps("o0")
     gg.d()
+    ox, oz = feat // 4, (feat // 2) % 2
+    os = jnp.where(oz == zh, 0, 1)
+    bd = bdec[...].reshape(1, 512)
+    for j in range(4):
+        q = (feat % 2) * 4 + j
+        pb = q + os * (1 - 2 * (q % 2))
+        xs = X[pb, os, ox].reshape(128, ROWS).astype(F32).T
+        errb[:, j * 128:(j + 1) * 128] = xs - bd[:, j * 128:(j + 1) * 128]
     cp.arrived("acts", apeer, d_core)
-    cp.arrived("wpeer0", wpeer.at[pl.ds(0, 4)], d_core)
-    cp.arrived("wpeer1", wpeer.at[pl.ds(4, 4)], d_core)
+    cp.arrived("wpeer", wpeer, d_core)
 
     def shares(name, lo, n):
         with mark(name):
@@ -384,17 +390,12 @@
     gg.h()
     gg.steps("op0", "zu1c", "zd1c", "zo1c", "opz")
     with mark("err"):
-        ox, oz = feat // 4, (feat // 2) % 2
-        os = jnp.where(oz == zh, 0, 1)
         term = jnp.zeros((ROWS, 128), F32)
-        bd = bdec[...].reshape(1, 512)
         for j in range(4):
             q = (feat % 2) * 4 + j
             pb = q + os * (1 - 2 * (q % 2))
-            xs = X[pb, os, ox].reshape(128, ROWS).astype(F32).T - bd[:, j * 128:(j + 1) * 128]
             gs = G[pb, os, ox].reshape(128, ROWS).astype(F32).T
-            errb[:, j * 128:(j + 1) * 128] = xs
-            term = term + xs * gs
+            term = term + errb[:, j * 128:(j + 1) * 128] * gs
         for j in range(5):
             lanes = slice(j * 128, (j + 1) * 128)
             f = acts[:, lanes].astype(F32) * projt[lanes, :].T

time: 55.7 us -> 55.7 us (level)
  no operation moved by 1% of the time
where the time goes in v7:
time: 55.7 us; the launch traced here: 55.6 us
  Pallas kernels  54.9 us (99%)
  between operations  0.64 us (1%)
    pallas_call x1, Pallas kernels, per_device(): pl.pallas_call(kernel, out_shape=tuple((V(*o) for o in outs)), in_specs=[...  53.9 us

profile of v7, /device:TPU:0, one launch (start us, length us, event | category | flops | bytes accessed | tf_op | source)
XLA Modules:
  0.0 55.6 jit_solution(4073470601989929656)
XLA Ops:
  0.6 53.9 %shard_map.94 = (f32[256,640]{1,0:T(8,128)S(1)}, f32[256,512]{1,0:T(8,128)S(1)}, f32[1,256]{1,0:T(1,128)S(1)}) custom-call(bf16[64,2048]{1,0:T(8,128)(2,1)} %bitcast.5, bf16[64,2048]{1,0:T(8,128)(2,1)} %bitcast.6, s32[2,20]{1,0:T(2,128)} %active_h.1, bf16[4,2,8,128,640]{4,3,2,1,0:T(8,128)(2,1)} %bitcast.4, f32[640]{0:T(1024)} %benc_h.1, ...), custom_call_target="tpu_custom_call" | custom-call | tf_op jit(solution)/shard_map/pallas_call | solution.py:456
  54.5 1.0 %shard_map.95 = (f32[256,640]{1,0:T(8,128)}, f32[256,512]{1,0:T(8,128)}, f32[1,256]{1,0:T(1,128)}) custom-call(f32[256,640]{1,0:T(8,128)S(1)} %get-tuple-element.9.fa, f32[256,512]{1,0:T(8,128)S(1)} %get-tuple-element.10.err, f32[1,256]{1,0:T(1,128)S(1)} %get-tuple-element.11.attr), custom_call_target="tpu_custom_call" | custom-call | tf_op jit(solution)/shard_map/pallas_call | solution.py:490
